TPU v7x, 512 devices: a whole 4x8x8 slice. The times are simulated.
512 devices in a mesh: roll: 64 (over y_hi, z, x), seq: 8 (over y_lo, core).
Axes of the slice: x: 4, y: 8 (y_hi: 2, y_lo: 4; y = y_hi * 4 + y_lo), z: 8, core: 2. Of those that a mesh axis runs over, the one named last changes fastest.
Arguments:
- hidden: bfloat16 [64, 4096, 2880], P('roll', 'seq'), may hold values from -6 to 6
- key_value_blocks: bfloat16 [2880, 1024], P('roll'), may hold values from -0.109375 to 0.109375
- block_of: int32 [64], replicated, may hold values from 0 to 63, each once
- queries: bfloat16 [64, 256, 4096], P('roll', 'seq'), may hold values from -480 to 480
- key_pos: int32 [64, 4096], P('roll', 'seq'), may hold values from 0 to 8190, as said below
- query_pos: int32 [64, 256], P('roll', 'seq'), may hold values from 0 to 8190, as said below
Outputs:
- context: bfloat16 [64, 256, 4096], P('roll', 'seq')
Inputs may be any that keep to these rules, and one draw needn't show every extreme that they name: Along each sequence key_pos rises by one from that sequence's start; starts lie in 0 to 4095 and some sequence starts at 0, another at 4095. `query_pos`: each query position lies between the first and the last key position of its sequence.
All inputs are finite; a program needn't handle non-finite values.
Results may differ from a plain program's by a relative error of at most 0.017.
The roundings to bfloat16 on the way count: a program that leaves them out, or rounds other values in their place, can miss the bound.
Values may be sent and summed in bfloat16 or wider, within the bound.
No kernel may reach another device: no remote copies, remote signals or barrier semaphores. Data moves between devices by JAX's collectives and lax.ppermute only.
A program may use at most 64 MiB of HBM per device.

v0:
```python
import math

import jax
import jax.numpy as jnp
from jax import lax
from jax.sharding import PartitionSpec as P

QUERY_HEAD_COUNT = 64
HEAD_WIDTH = 64


rope_base = 150000.0


def rotary(vectors, positions):
    head_size = vectors.shape[-1]
    half = head_size // 2
    freq = rope_base ** (-(jnp.arange(half).astype(jnp.float32) * 2.0 / head_size))
    angle = positions.astype(jnp.float32)[:, None] * freq[None, :]
    cosine = jnp.cos(angle)[:, None, :]
    sine = jnp.sin(angle)[:, None, :]
    first = vectors[..., :half]
    second = vectors[..., half:]
    return jnp.concatenate(
        [first * cosine - second * sine, second * cosine + first * sine], axis=-1
    )


def shards(hidden, key_value_blocks, block_of, queries, key_pos, query_pos):
    local_rows = hidden[0]
    row_count = local_rows.shape[0]
    block_rows = key_value_blocks.shape[0]
    all_columns = key_value_blocks.shape[1]
    seq_devices = lax.axis_size("seq")
    kv_heads_all = all_columns // (2 * HEAD_WIDTH)
    local_heads = kv_heads_all // seq_devices
    query_group = QUERY_HEAD_COUNT // kv_heads_all
    query_local = queries[0]
    query_count = query_local.shape[0]
    rotated_rows = rotary(
        query_local.astype(jnp.float32).reshape(query_count, QUERY_HEAD_COUNT, HEAD_WIDTH),
        query_pos[0],
    )
    rotated_rows = rotated_rows.astype(jnp.bfloat16).reshape(
        query_count, kv_heads_all, query_group * HEAD_WIDTH
    )
    piece = lax.all_gather(key_value_blocks, "roll", axis=0, tiled=True)
    count = piece.shape[0] // block_rows

    def one_block(offset, accum):
        logical = block_of[offset]
        hidden_cols = lax.dynamic_slice_in_dim(local_rows, logical * block_rows, block_rows, 1)
        weight_rows = lax.dynamic_slice_in_dim(piece, offset * block_rows, block_rows, 0)
        return accum + jnp.dot(hidden_cols, weight_rows, preferred_element_type=jnp.float32)

    projected_rows = lax.fori_loop(
        0, count, one_block, jnp.zeros((row_count, all_columns), jnp.float32)
    )
    projected_rows = projected_rows.reshape(row_count, kv_heads_all, 2 * HEAD_WIDTH)
    keys = rotary(projected_rows[..., :HEAD_WIDTH], key_pos[0]).astype(jnp.bfloat16)
    values = projected_rows[..., HEAD_WIDTH:].astype(jnp.bfloat16)
    packed = jnp.concatenate([keys, values], axis=-1)
    kv_local, query_heads = (
        lax.all_to_all(packed, "seq", split_axis=1, concat_axis=0, tiled=True),
        lax.all_to_all(rotated_rows, "seq", split_axis=1, concat_axis=0, tiled=True),
    )
    all_key_pos, all_query_pos = (
        lax.all_gather(key_pos[0], "seq", axis=0, tiled=True),
        lax.all_gather(query_pos[0], "seq", axis=0, tiled=True),
    )
    total_queries = query_heads.shape[0]
    block_queries = math.gcd(total_queries, 64)
    block_count = total_queries // block_queries
    scale = 1.0 / jnp.sqrt(jnp.float32(HEAD_WIDTH))

    def attend(index):
        head = index // block_count
        block = index % block_count
        query_block = lax.dynamic_slice(
            query_heads,
            (block * block_queries, head, 0),
            (block_queries, 1, query_group * HEAD_WIDTH),
        )
        query_block = query_block.reshape(block_queries * query_group, HEAD_WIDTH)
        head_kv = lax.dynamic_index_in_dim(kv_local, head, 1, False)
        positions = lax.dynamic_slice_in_dim(all_query_pos, block * block_queries, block_queries)
        row_pos = jnp.repeat(positions, query_group)
        scores = (
            lax.dot_general(
                query_block,
                head_kv[:, :HEAD_WIDTH],
                (((1,), (1,)), ((), ())),
                preferred_element_type=jnp.float32,
            )
            * scale
        )
        allowed = all_key_pos[None, :] <= row_pos[:, None]
        scores = jnp.where(allowed, scores, -1e30)
        top = jnp.max(scores, axis=1, keepdims=True)
        expo = jnp.where(allowed, jnp.exp(scores - top), 0.0)
        probs = (expo / jnp.sum(expo, axis=1, keepdims=True)).astype(jnp.bfloat16)
        result = jnp.dot(probs, head_kv[:, HEAD_WIDTH:], preferred_element_type=jnp.float32).astype(
            jnp.bfloat16
        )
        return result.reshape(block_queries, query_group * HEAD_WIDTH)

    outputs = lax.map(attend, jnp.arange(local_heads * block_count))
    outputs = outputs.reshape(
        local_heads, block_count, block_queries, query_group * HEAD_WIDTH
    ).transpose(1, 2, 0, 3)
    outputs = outputs.reshape(total_queries, local_heads, query_group * HEAD_WIDTH)
    returned = lax.all_to_all(outputs, "seq", split_axis=0, concat_axis=1, tiled=True)
    return returned.reshape(1, query_count, QUERY_HEAD_COUNT * HEAD_WIDTH)


def solution(mesh):
    return jax.shard_map(
        shards,
        mesh=mesh,
        in_specs=(
            P("roll", "seq", None),
            P("roll", None),
            P(),
            P("roll", "seq", None),
            P("roll", "seq"),
            P("roll", "seq"),
        ),
        out_specs=P("roll", "seq", None),
        check_vma=False,
    )
```

profile of v0, /device:TPU:1, one launch (start us, length us, event | category | flops | bytes accessed | tf_op | source)
XLA Modules:
  0.0 524.1 jit_solution(15768045203367563707)
XLA Ops:
  8.0 4.6 copy.26
  12.9 165.3 %all-gather.5.cloned.1.call-done = bf16[64,45,1024]{2,1,0:T(8,128)(2,1)} async-done(((bf16[1,45,1024]{2,1,0:T(8,128)(2,1)}), bf16[64,45,1024]{2,1,0:T(8,128)(2,1)}) %all-gather.5.cloned.1.call-update) | async-done | bytes 5898256 | tf_op jit(solution)/shard_map/all_gather | solution.py:47
  178.2 8.3 %reshape.151 = bf16[2880,1024]{1,0:T(8,128)(2,1)} reshape(bf16[64,45,1024]{2,1,0:T(8,128)(2,1)} %all-gather.5.cloned.1.call-done) | data formatting | bytes 11796480
  186.6 199.2 %while.27 = (s32[]{:T(128)}, f32[512,1024]{1,0:T(8,128)S(1)}, s32[64]{0:T(128)S(1)}, bf16[512,2880]{1,0:T(8,128)(2,1)}, bf16[2880,1024]{1,0:T(8,128)(2,1)}, /*in...) while((s32[]{:T(128)}, f32[512,1024]{1,0:T(8,128)S(1)}, s32[64]{0:T(128)S(1)}, ...), condition=%wide.region_1.0_spmd.clone, body=%wide.region_0.0_spmd.clone.sunk | while | flops 48234504 | bytes 4423903 | solution.py:56
  188.0 1.7 select_add_fusion.2
  194.2 1.7 select_add_fusion.2
  197.3 1.7 select_add_fusion.2
  212.9 1.7 select_add_fusion.2
  216.0 1.7 select_add_fusion.2
  225.3 1.7 select_add_fusion.2
  240.9 1.7 select_add_fusion.2
  244.0 1.7 select_add_fusion.2
  253.3 1.7 select_add_fusion.2
  259.5 1.7 select_add_fusion.2
  268.9 1.7 select_add_fusion.2
  272.0 1.7 select_add_fusion.2
  385.8 1.9 copy.27
  391.4 15.6 %all-to-all-start.1 = ((bf16[512,8,128]{0,2,1:T(8,128)(2,1)}), bf16[512,8,128]{0,2,1:T(8,128)(2,1)S(1)}, u32[]{:S(2)}, u32[]{:S(2)}) async-start(bf16[512,8,128]{0,2,1:T(8,128)(2,1)} %pad_maximum_fusion), calls=%async_computation.1 | async-start | bytes 2097152 | tf_op jit(solution)/shard_map/all_to_all | solution.py:64
  409.5 23.1 %all-to-all-done.1 = bf16[512,8,128]{0,2,1:T(8,128)(2,1)S(1)} async-done(((bf16[512,8,128]{0,2,1:T(8,128)(2,1)}), bf16[512,8,128]{0,2,1:T(8,128)(2,1)S(1)}, u32[]{:S(2)}, u32[]{:S(2)}) %all-to-all-start.1) | async-done | bytes 1048608 | tf_op jit(solution)/shard_map/all_to_all | solution.py:64
  432.6 4.3 all-to-all-start
  438.8 7.7 %all-reduce = s32[256]{0:T(256)S(1)} all-reduce(s32[256]{0:T(256)S(1)} %bitcast_dynamic-update-slice_fusion), channel_id=3, replica_groups=mesh['roll'=64,'seq'=8] {'seq'}, use_global_device_ids=true, to_apply=%add | all-reduce | flops 256 | bytes 2048 | tf_op jit(solution)/shard_map/all_gather | solution.py:69
  446.6 14.4 %all-gather = s32[1,4096]{1,0:T(1,128)S(1)} all-gather(s32[1,512]{1,0:T(1,128)S(1)} %copy-done.1), channel_id=2, replica_groups=mesh['roll'=64,'seq'=8] {'seq'}, dimensions={1}, use_global_device_ids=true | all-gather | bytes 18432 | tf_op jit(solution)/shard_map/all_gather | solution.py:68
  461.7 41.5 %while.26 = (s32[]{:T(128)}, bf16[4,64,512]{2,1,0:T(8,128)(2,1)S(1)}, s32[4096]{0:T(1024)S(1)}, s32[4]{0:T(128)S(1)}, s32[256]{0:T(256)S(1)}, /*index=5*/bf16[25...) while((s32[]{:T(128)}, ...), condition=%wide.region_5.6_spmd, body=%wide.region_2.5_spmd.sunk | while | flops 572554240 | bytes 28122160 | solution.py:107
  466.1 2.6 fusion.24
  468.7 3.0 fusion.25
  476.5 2.6 fusion.24
  479.1 3.0 fusion.25
  486.8 2.6 fusion.24
  489.5 3.0 fusion.25
  497.2 2.6 fusion.24
  499.8 3.0 fusion.25
  504.7 11.3 %all_to_all.51 = bf16[8,2,8192]{2,1,0:T(2,128)(2,1)S(1)} all-to-all(bf16[8,2,8192]{2,1,0:T(2,128)(2,1)S(1)} %reshape.155), channel_id=1, replica_groups=mesh['roll'=64,'seq'=8] {'seq'}, dimensions={0} | all-to-all | bytes 524288 | tf_op jit(solution)/shard_map/all_to_all | solution.py:112
  (194 shorter events, 155.1 us)
Async XLA Ops:
  6.5 171.7 %all-gather.5.cloned.1.call-start = ((), (), s32[]{:S(2)}) async-start(), calls=%async_computation.3 | async-start | bytes 6389760 | tf_op jit(solution)/shard_map/all_gather | solution.py:47
  8.0 178.6 %copy-start.2 = (s32[64]{0:T(128)S(1)}, s32[64]{0:T(128)}, u32[]{:S(2)}) copy-start(s32[64]{0:T(128)} %param.12) | copy-start | bytes 772
  385.8 21.2 %copy-start = (bf16[1,32,4096]{2,1,0:T(8,128)(2,1)S(1)}, bf16[1,32,4096]{2,1,0:T(8,128)(2,1)}, u32[]{:S(2)}) copy-start(bf16[1,32,4096]{2,1,0:T(8,128)(2,1)} %param.13) | copy-start | bytes 786436
  385.8 21.6 %copy-start.3 = (s32[1,32]{1,0:T(1,128)S(1)}, s32[1,32]{1,0:T(1,128)}, u32[]{:S(2)}) copy-start(s32[1,32]{1,0:T(1,128)} %param.15) | copy-start | bytes 388
  387.7 58.9 %copy-start.1 = (s32[1,512]{1,0:T(1,128)S(1)}, s32[1,512]{1,0:T(1,128)}, u32[]{:S(2)}) copy-start(s32[1,512]{1,0:T(1,128)} %param.14) | copy-start | bytes 6148
  391.4 41.2 %all-to-all-start.1 = ((bf16[512,8,128]{0,2,1:T(8,128)(2,1)}), bf16[512,8,128]{0,2,1:T(8,128)(2,1)S(1)}, u32[]{:S(2)}, u32[]{:S(2)}) async-start(bf16[512,8,128]{0,2,1:T(8,128)(2,1)} %pad_maximum_fusion), calls=%async_computation.1 | async-start | bytes 2097152 | tf_op jit(solution)/shard_map/all_to_all | solution.py:64
  432.6 29.0 %all-to-all-start = ((bf16[32,8,512]{2,0,1:T(8,128)(2,1)}), bf16[32,8,512]{2,0,1:T(8,128)(2,1)S(1)}, u32[]{:S(2)}, u32[]{:S(2)}) async-start(bf16[32,8,512]{2,0,1:T(8,128)(2,1)} %copy.25), calls=%async_computation | async-start | bytes 524288 | tf_op jit(solution)/shard_map/all_to_all | solution.py:65
Sparse Core Ops, SparseCore 0:
  11.9 166.3 all-gather.4
where the time goes:
time: 527 us; the launch traced here: 524 us
  waiting for transfers between devices  189 us (36%)
  matrix products  128 us (24%)
  local copies, waits for them, and re-layouts  69.3 us (13%)
  loops' own time  55 us (10%)
  blocking collectives  33.4 us (6%)
  starting transfers between devices  19.9 us (4%)
  other arithmetic  15.7 us (3%)
  between operations  14.1 us (3%)
    all_gather x1, waiting for transfers between devices, shards(): piece = lax.all_gather(key_value_blocks, 'roll', axis=0, tiled=True)  165 us
    dot_general x64, matrix products, one_block(): jnp.dot(hidden_cols, weight_rows, preferred_element_type=jnp.float32)  110 us
    another operation x1, loops' own time, shards(): lax.fori_loop(0, count, one_block, jnp.zeros((row_count, all_columns), jn...  47 us
    dynamic_slice x64, local copies, waits for them, and re-layouts, one_block(): logical = block_of[offset]  42.6 us
    all_to_all x1, waiting for transfers between devices, shards(): lax.all_to_all(packed, 'seq', split_axis=1, concat_axis=0, tiled=True)  23.1 us
    all_to_all x1, starting transfers between devices, shards(): lax.all_to_all(packed, 'seq', split_axis=1, concat_axis=0, tiled=True)  15.6 us
    unnamed x16, local copies, waits for them, and re-layouts  14.8 us
    all_gather x1, blocking collectives, shards(): lax.all_gather(key_pos[0], 'seq', axis=0, tiled=True)  14.4 us
  transfers between devices with their start and end apart: 3, of which 2 were waited for; matrix products, arithmetic and copies ran while one was open for 2% of the time, Pallas kernels for 0%

commit v1 on v0

v1 whole, which is shorter than its diff:
```python
import functools

import jax
import jax.numpy as jnp
import numpy as np
from jax import lax
from jax.experimental import pallas as pl
from jax.experimental.pallas import tpu as pltpu
from jax.sharding import Mesh, PartitionSpec as P

HEADS = 64
KV_HEADS = 8
WIDTH = 64
GROUP = HEADS // KV_HEADS
LANES = 2 * WIDTH
ROPE_BASE = 150000.0
PAD_ROWS = 48
QUERY_BLOCK = 32
KEY_BLOCK = 512
ROLL = ("yh", "z", "x")
SEQ = ("yl", "co")


def lane_frequencies(lanes):
    half = WIDTH // 2
    freq = ROPE_BASE ** (-(jnp.arange(half).astype(jnp.float32) * 2.0 / WIDTH))
    return jnp.tile(freq, lanes // half)


def ring(size, step):
    return [(i, (i + step) % size) for i in range(size)]


def reorder_kernel(source_ref, hidden_ref, out_ref):
    depth = hidden_ref.shape[1]
    index = lax.broadcasted_iota(jnp.int32, (depth, source_ref.shape[1]), 0)
    pick = jnp.where(index == source_ref[...], 1.0, 0.0).astype(jnp.bfloat16)
    out_ref[...] = jnp.dot(
        hidden_ref[...], pick, preferred_element_type=jnp.float32
    ).astype(jnp.bfloat16)


def reorder(hidden, source):
    rows, depth = hidden.shape
    columns = source.shape[1]
    tile = 256
    return pl.pallas_call(
        reorder_kernel,
        grid=(columns // tile,),
        in_specs=[
            pl.BlockSpec((1, tile), lambda i: (0, i)),
            pl.BlockSpec((rows, depth), lambda i: (0, 0)),
        ],
        out_specs=pl.BlockSpec((rows, tile), lambda i: (0, i)),
        out_shape=jax.ShapeDtypeStruct((rows, columns), jnp.bfloat16),
        name="reorder_hidden",
    )(source, hidden)


def swap_halves(x, lane):
    half = WIDTH // 2
    return jnp.where(
        lane % WIDTH < half,
        pltpu.roll(x, LANES - half, 1),
        pltpu.roll(x, half, 1),
    )


def project_kernel(core_ref, own_ref, other_ref, *rest):
    pieces, (cos_ref, sin_ref, out_ref) = rest[:-3], rest[-3:]
    rows = own_ref.shape[0]
    core = core_ref[0]
    lane = lax.broadcasted_iota(jnp.int32, (rows, LANES), 1)
    for hidden_ref, place in ((own_ref, core), (other_ref, 1 - core)):
        total = None
        offset = 0
        for piece in pieces:
            size = piece.shape[0]
            part = jnp.dot(
                hidden_ref[:, offset : offset + size],
                piece[...],
                preferred_element_type=jnp.float32,
            )
            total = part if total is None else total + part
            offset += size
        base = pl.multiple_of(place * rows, rows)
        cosine = cos_ref[pl.ds(base, rows), :]
        sine = sin_ref[pl.ds(base, rows), :]
        for head in range(out_ref.shape[0]):
            x = total[:, head * LANES : (head + 1) * LANES]
            out_ref[head, pl.ds(base, rows), :] = (
                x * cosine + swap_halves(x, lane) * sine
            ).astype(jnp.bfloat16)


def project(core, own, other, pieces, cosine, sine):
    rows = own.shape[0]
    heads = pieces[0].shape[1] // LANES
    vmem = pl.BlockSpec(memory_space=pltpu.VMEM)
    return pl.pallas_call(
        project_kernel,
        in_specs=[pl.BlockSpec(memory_space=pltpu.SMEM)] + [vmem] * (len(pieces) + 4),
        out_specs=vmem,
        out_shape=jax.ShapeDtypeStruct((heads, 2 * rows, LANES), jnp.bfloat16),
        name="project",
    )(core, own, other, *pieces, cosine, sine)


def prepare_kernel(query_ref, pick_ref, cos_ref, sin_ref, out_ref):
    rows = query_ref.shape[0]
    lane = lax.broadcasted_iota(jnp.int32, (rows, LANES), 1)
    pick = pick_ref[...]
    for pair in range(GROUP // 2):
        x = jnp.dot(
            pick,
            query_ref[:, pair * LANES : (pair + 1) * LANES],
            preferred_element_type=jnp.float32,
        )
        x = x * cos_ref[...] + swap_halves(x, lane) * sin_ref[...]
        x = x.astype(jnp.bfloat16).astype(jnp.float32) * (1.0 / 8.0)
        first = jnp.where(lane < WIDTH, x, 0.0).astype(jnp.bfloat16)
        second = jnp.where(lane < WIDTH, pltpu.roll(x, WIDTH, 1), 0.0).astype(jnp.bfloat16)
        for block in range(rows // QUERY_BLOCK):
            here = slice(block * QUERY_BLOCK, (block + 1) * QUERY_BLOCK)
            for head, value in ((2 * pair, first), (2 * pair + 1, second)):
                out_ref[block, head * QUERY_BLOCK : (head + 1) * QUERY_BLOCK, :] = value[here]


def prepare(query, pick, cosine, sine):
    rows = query.shape[0]
    vmem = pl.BlockSpec(memory_space=pltpu.VMEM)
    return pl.pallas_call(
        prepare_kernel,
        in_specs=[vmem] * 4,
        out_specs=vmem,
        out_shape=jax.ShapeDtypeStruct(
            (rows // QUERY_BLOCK, GROUP * QUERY_BLOCK, LANES), jnp.bfloat16
        ),
        name="prepare_queries",
    )(query, pick, cosine, sine)


def attend_kernel(
    bound_ref, query_ref, kv_ref, last_ref, unpick_ref, out_ref, value_ref, sorted_ref
):
    blocks = query_ref.shape[0]
    rows = query_ref.shape[1]
    keys = kv_ref.shape[0]
    lane_kv = lax.broadcasted_iota(jnp.int32, (KEY_BLOCK, LANES), 1)
    for step in range(keys // KEY_BLOCK):
        here = slice(step * KEY_BLOCK, (step + 1) * KEY_BLOCK)
        value_ref[here, :] = jnp.where(
            lane_kv < WIDTH, jnp.ones((), jnp.bfloat16), kv_ref[here, :]
        )
    column = lax.broadcasted_iota(jnp.int32, (rows, KEY_BLOCK), 1)
    lane = lax.broadcasted_iota(jnp.int32, (QUERY_BLOCK, LANES), 1)

    def one_block(block, carry):
        query = query_ref[block]
        last = last_ref[block]

        def step(masked, index, state):
            top, total = state
            base = pl.multiple_of(index * KEY_BLOCK, KEY_BLOCK)
            scores = lax.dot_general(
                query,
                kv_ref[pl.ds(base, KEY_BLOCK), :],
                (((1,), (1,)), ((), ())),
                preferred_element_type=jnp.float32,
            )
            if masked:
                scores = jnp.where(column <= last - base, scores, -1e30)
            new_top = jnp.maximum(top, jnp.max(scores, axis=1, keepdims=True))
            expo = jnp.exp(scores - new_top)
            part = jnp.dot(
                expo.astype(jnp.bfloat16),
                value_ref[pl.ds(base, KEY_BLOCK), :],
                preferred_element_type=jnp.float32,
            )
            return new_top, total * jnp.exp(top - new_top) + part

        state = (
            jnp.full((rows, 1), -1e30, jnp.float32),
            jnp.zeros((rows, LANES), jnp.float32),
        )
        full = bound_ref[0, block]
        state = lax.fori_loop(0, full, functools.partial(step, False), state)
        _, total = lax.fori_loop(full, bound_ref[1, block], functools.partial(step, True), state)
        result = total / pltpu.roll(total, WIDTH, 1)
        place = pl.multiple_of(block * QUERY_BLOCK, QUERY_BLOCK)
        for pair in range(GROUP // 2):
            even = result[2 * pair * QUERY_BLOCK : (2 * pair + 1) * QUERY_BLOCK]
            odd = result[(2 * pair + 1) * QUERY_BLOCK : (2 * pair + 2) * QUERY_BLOCK]
            sorted_ref[pl.ds(place, QUERY_BLOCK), pair * LANES : (pair + 1) * LANES] = jnp.where(
                lane < WIDTH, pltpu.roll(even, WIDTH, 1), odd
            ).astype(jnp.bfloat16)
        return carry

    lax.fori_loop(0, blocks, one_block, 0)
    out_ref[...] = jnp.dot(
        unpick_ref[...], sorted_ref[...], preferred_element_type=jnp.float32
    ).astype(jnp.bfloat16)


def attend(bounds, query, kv, last, unpick):
    vmem = pl.BlockSpec(memory_space=pltpu.VMEM)
    count = unpick.shape[0]
    return pl.pallas_call(
        attend_kernel,
        in_specs=[pl.BlockSpec(memory_space=pltpu.SMEM)] + [vmem] * 4,
        out_specs=vmem,
        out_shape=jax.ShapeDtypeStruct((count, GROUP * WIDTH), jnp.bfloat16),
        scratch_shapes=[
            pltpu.VMEM(kv.shape, jnp.bfloat16),
            pltpu.VMEM((count, GROUP * WIDTH), jnp.bfloat16),
        ],
        name="attend",
    )(bounds, query, kv, last, unpick)


def gather_weight(blocks):
    block_rows = blocks.shape[0]
    core = lax.axis_index("co")
    split = blocks.reshape(block_rows, KV_HEADS // 2, 2, LANES)
    mine = lax.dynamic_index_in_dim(split, core, 2, False).reshape(block_rows, -1)
    mine = jnp.pad(mine, ((0, PAD_ROWS - block_rows), (0, 0)))
    far = lax.ppermute(mine, "yh", ring(2, 1))
    both = jnp.concatenate([mine, far], 0)
    plane = lax.all_to_all(
        jnp.broadcast_to(both[None], (8,) + both.shape), "z", 0, 0, tiled=True
    )
    plane = plane.reshape(8 * 2 * PAD_ROWS, -1)
    half = plane.shape[0] // 2
    below = lax.ppermute(plane, "x", ring(4, 1))
    above = lax.ppermute(plane, "x", ring(4, -1))
    across_low = lax.ppermute(below[:half], "x", ring(4, 1))
    across_high = lax.ppermute(above[half:], "x", ring(4, -1))
    return plane, below, above, across_low, across_high


def slot_order(block_of):
    yh, z, x = (lax.axis_index(a) for a in ROLL)
    xs = jnp.stack([x, x + 3, x + 1, x + 2]) % 4
    ys = jnp.stack([yh, 1 - yh])
    stored = (
        ys[None, None, :] * 32 + jnp.arange(8)[None, :, None] * 4 + xs[:, None, None]
    ).reshape(-1)
    return block_of[stored]


def shards(hidden, blocks, block_of, queries, key_pos, query_pos):
    core = lax.axis_index("co")
    seq_index = lax.axis_index(SEQ)
    seq = lax.axis_size(SEQ)
    rows = hidden.shape[1]
    keys = rows * seq
    block_rows = blocks.shape[0]
    query_rows = queries.shape[1]
    start = key_pos[0, 0] - rows * seq_index

    slots = slot_order(block_of)
    inner = jnp.arange(PAD_ROWS)
    source = jnp.where(
        inner[None, :] < block_rows, slots[:, None] * block_rows + inner[None, :], -1
    ).reshape(1, -1)

    high = (query_pos[0] >> 8).astype(jnp.bfloat16)
    low = (query_pos[0] & 255).astype(jnp.bfloat16)
    extra = jnp.concatenate(
        [
            jnp.broadcast_to(high[:, None, None], (query_rows, KV_HEADS, WIDTH)),
            jnp.broadcast_to(low[:, None, None], (query_rows, KV_HEADS, WIDTH)),
        ],
        -1,
    )
    payload = jnp.concatenate([queries[0].reshape(query_rows, KV_HEADS, GROUP * WIDTH), extra], -1)
    payload = lax.all_to_all(payload.transpose(1, 0, 2), SEQ, 0, 0, tiled=True)

    pieces = gather_weight(blocks)
    own = reorder(hidden[0], source)
    other = lax.ppermute(own, "co", ring(2, 1))

    total_queries = query_rows * seq
    payload = payload.reshape(total_queries, -1)
    query = payload[:, : GROUP * WIDTH]
    positions = (
        payload[:, GROUP * WIDTH].astype(jnp.float32) * 256.0
        + payload[:, GROUP * WIDTH + WIDTH].astype(jnp.float32)
    ).astype(jnp.int32)
    order = jnp.arange(total_queries)
    before = (positions[None, :] < positions[:, None]) | (
        (positions[None, :] == positions[:, None]) & (order[None, :] < order[:, None])
    )
    rank = jnp.sum(before.astype(jnp.int32), axis=1)
    pick_mask = rank[None, :] == order[:, None]
    sorted_pos = jnp.sum(jnp.where(pick_mask, positions[None, :], 0), axis=1)
    pick = pick_mask.astype(jnp.bfloat16)
    unpick = (rank[:, None] == order[None, :]).astype(jnp.bfloat16)
    last = sorted_pos - start
    by_block = last.reshape(-1, QUERY_BLOCK)
    bounds = jnp.stack(
        [(by_block[:, 0] + 1) // KEY_BLOCK, by_block[:, -1] // KEY_BLOCK + 1]
    )
    last_rows = jnp.tile(by_block, (1, GROUP))[..., None]

    sign = jnp.asarray(np.where(np.arange(LANES) % WIDTH < WIDTH // 2, -1.0, 1.0), jnp.float32)
    freq = lane_frequencies(LANES)
    query_angle = sorted_pos.astype(jnp.float32)[:, None] * freq[None, :]
    prepared = prepare(query, pick, jnp.cos(query_angle), jnp.sin(query_angle) * sign)

    is_key = jnp.arange(LANES) < WIDTH
    chip_rows = 2 * rows
    chip_pos = start + chip_rows * lax.axis_index("yl") + jnp.arange(chip_rows)
    key_angle = chip_pos.astype(jnp.float32)[:, None] * jnp.where(is_key, freq, 0.0)[None, :]
    key_sine = jnp.sin(key_angle) * jnp.where(is_key, sign, 0.0)

    kv = project(core.reshape(1), own, other, pieces, jnp.cos(key_angle), key_sine)
    kv = lax.all_to_all(kv, "yl", 0, 0, tiled=True).reshape(keys, LANES)
    context = attend(bounds, prepared, kv, last_rows, unpick)
    context = context.reshape(seq, query_rows, GROUP * WIDTH)
    context = lax.all_to_all(context, SEQ, 0, 0, tiled=True)
    return context.transpose(1, 0, 2).reshape(1, query_rows, HEADS * WIDTH)


def solution(mesh):
    fine = Mesh(mesh.devices.reshape(2, 8, 4, 4, 2), ROLL + SEQ)
    return jax.shard_map(
        shards,
        mesh=fine,
        in_specs=(
            P(ROLL, SEQ, None),
            P(ROLL, None),
            P(),
            P(ROLL, SEQ, None),
            P(ROLL, SEQ),
            P(ROLL, SEQ),
        ),
        out_specs=P(ROLL, SEQ, None),
        check_vma=False,
    )
```

time: 527 us -> 182 us (0.35)
  waiting for transfers between devices: 189 us -> 26.5 us
  matrix products: 128 us -> 0 us
  loops' own time: 55 us -> 0 us
  local copies, waits for them, and re-layouts: 69.3 us -> 15.7 us
  Pallas kernels: 0 us -> 50.7 us
  starting transfers between devices: 19.9 us -> 37.8 us
  between operations: 14.1 us -> 0.95 us
  other arithmetic: 15.7 us -> 7.58 us
  blocking collectives: 33.4 us -> 40.8 us
    all_gather x1 -> x0, waiting for transfers between devices: 165 us -> none  [shards(): piece = lax.all_gather(key_value_blocks, 'roll', axis=0, tiled=True)]
    dot_general x72 -> x0, matrix products: 128 us -> none  [the longest x64 110 us: one_block(): jnp.dot(hidden_cols, weight_rows, preferred_element_type=jnp.float32)]
    another operation x2 -> x0, loops' own time: 55 us -> none  [the longest x1 47 us: shards(): lax.fori_loop(0, count, one_block, jnp.zeros((row_count, all_columns), jn...]
    pallas_call x0 -> x4, Pallas kernels: none -> 50.7 us  [the longest x1 24.4 us: attend(): pl.pallas_call(attend_kernel, in_specs=[pl.BlockSpec(memory_space=pltpu.S...]
    dynamic_slice x76 -> x1, local copies, waits for them, and re-layouts: 45.4 us -> 0.29 us  [gather_weight(): lax.dynamic_index_in_dim(split, core, 2, False).reshape(block_rows, -1)]
    all_to_all x1 -> x2, blocking collectives: 11.3 us -> 40.8 us  [the longest x1 26.4 us: gather_weight(): lax.all_to_all(jnp.broadcast_to(both[None], (8,) + both.shape), 'z', 0, 0...]
    ppermute x0 -> x6, starting transfers between devices: none -> 23.9 us  [the longest x1 8.87 us: shards(): other = lax.ppermute(own, 'co', ring(2, 1))]
    all_gather x2 -> x0, blocking collectives: 22.2 us -> none  [the longest x1 14.4 us: shards(): lax.all_gather(key_pos[0], 'seq', axis=0, tiled=True)]
  transfers between devices with their start and end apart: 3 -> 8, of which waited for: 2 -> 4; matrix products, arithmetic and copies ran while one was open for 2% -> 8% of each run, Pallas kernels for 0% -> 6%
where the time goes in v1:
time: 182 us; the launch traced here: 180 us
  Pallas kernels  50.7 us (28%)
  blocking collectives  40.8 us (22%)
  starting transfers between devices  37.8 us (21%)
  waiting for transfers between devices  26.5 us (15%)
  local copies, waits for them, and re-layouts  15.7 us (9%)
  other arithmetic  7.58 us (4%)
    all_to_all x1, blocking collectives, gather_weight(): lax.all_to_all(jnp.broadcast_to(both[None], (8,) + both.shape), 'z', 0, 0...  26.4 us
    pallas_call x1, Pallas kernels, attend(): pl.pallas_call(attend_kernel, in_specs=[pl.BlockSpec(memory_space=pltpu.S...  24.4 us
    all_to_all x1, waiting for transfers between devices, shards(): kv = lax.all_to_all(kv, 'yl', 0, 0, tiled=True).reshape(keys, LANES)  15.6 us
    pallas_call x1, Pallas kernels, reorder(): pl.pallas_call(reorder_kernel, grid=(columns // tile,), in_specs=[pl.Bloc...  14.7 us
    all_to_all x1, blocking collectives, shards(): context = lax.all_to_all(context, SEQ, 0, 0, tiled=True)  14.4 us
    pallas_call x1, Pallas kernels, project(): pl.pallas_call(project_kernel, in_specs=[pl.BlockSpec(memory_space=pltpu....  9.12 us
    ppermute x1, starting transfers between devices, shards(): other = lax.ppermute(own, 'co', ring(2, 1))  8.87 us
    all_to_all x1, starting transfers between devices, shards(): payload = lax.all_to_all(payload.transpose(1, 0, 2), SEQ, 0, 0, tiled=True)  8.02 us
  transfers between devices with their start and end apart: 8, of which 4 were waited for; matrix products, arithmetic and copies ran while one was open for 8% of the time, Pallas kernels for 6%

profile of v1, /device:TPU:1, one launch (start us, length us, event | category | flops | bytes accessed | tf_op | source)
XLA Modules:
  0.0 180.0 jit_solution(12176725957735553346)
XLA Ops:
  0.7 0.8 gather_fusion
  1.5 0.7 select_n.83.source_ref
  2.2 4.6 %copy.23 = bf16[1,512,2880]{2,1,0:T(8,128)(2,1)} copy(bf16[1,512,2880]{1,2,0:T(8,128)(2,1)} %param.7) | data formatting | bytes 5898240 | tf_op args[0]
  6.8 14.7 %reorder_hidden.1.own_ref = bf16[512,3072]{1,0:T(8,128)(2,1)} custom-call(s32[1,3072]{1,0:T(1,128)} %select_n.83.source_ref, bf16[512,2880]{1,0:T(8,128)(2,1)} %bitcast.46), custom_call_target="tpu_custom_call" | custom-call | tf_op jit(solution)/shard_map/reorder_hidden/pallas_call | solution.py:47
  21.5 8.9 %collective-permute-start = (bf16[512,3072]{1,0:T(8,128)(2,1)}, bf16[512,3072]{1,0:T(8,128)(2,1)}, u32[]{:S(2)}, u32[]{:S(2)}) collective-permute-start(bf16[512,3072]{1,0:T(8,128)(2,1)} %reorder_hidden.1.own_ref), channel_id=1, source_target_pairs={{0,1},{1,0},{2,3},{3,2},{4,5},{5,4},{6,7},{7,6},{8,9},{9,8},{10,11... | collective-permute-start | bytes 9437192 | tf_op jit(solution)/shard_map/ppermute | solution.py:281
  30.8 2.1 %collective-permute-start.1 = (bf16[48,512]{1,0:T(8,128)(2,1)S(1)}, bf16[48,512]{1,0:T(8,128)(2,1)S(1)}, u32[]{:S(2)}, u32[]{:S(2)}) collective-permute-start(bf16[48,512]{1,0:T(8,128)(2,1)S(1)} %pad.4), channel_id=1, source_target_pairs={{0,256},{256,0},{1,257},{257,1},{2,258},{258,2},{3,259},{259,3},{4... | collective-permute-start | bytes 147464 | tf_op jit(solution)/shard_map/ppermute | solution.py:227
  32.9 7.0 %collective-permute-done.1 = bf16[48,512]{1,0:T(8,128)(2,1)S(1)} collective-permute-done((bf16[48,512]{1,0:T(8,128)(2,1)S(1)}, bf16[48,512]{1,0:T(8,128)(2,1)S(1)}, u32[]{:S(2)}, u32[]{:S(2)}) %collective-permute-start.1) | collective-permute-done | bytes 49184 | tf_op jit(solution)/shard_map/ppermute | solution.py:227
  40.0 26.4 %all_to_all.20 = bf16[8,96,512]{2,1,0:T(8,128)(2,1)S(1)} all-to-all(bf16[8,96,512]{2,1,0:T(8,128)(2,1)S(1)} %broadcast_in_dim.33), channel_id=1, replica_groups=mesh['yh'=2,'z'=8,'x'=4,'yl'=4,'co'=2] {'z'}, dimensions={0} | all-to-all | bytes 1572864 | tf_op jit(solution)/shard_map/all_to_all | solution.py:229
  66.4 3.1 %collective-permute-start.2 = (bf16[768,512]{1,0:T(8,128)(2,1)S(1)}, bf16[768,512]{1,0:T(8,128)(2,1)S(1)}, u32[]{:S(2)}, u32[]{:S(2)}) collective-permute-start(bf16[768,512]{1,0:T(8,128)(2,1)S(1)} %bitcast.48), channel_id=1, source_target_pairs={{0,8},{8,16},{16,24},{24,0},{1,9},{9,17},{17,25},{25,1},{2,10},{10... | collective-permute-start | bytes 2359304 | tf_op jit(solution)/shard_map/ppermute | solution.py:234
  69.5 3.4 %collective-permute-start.3 = (bf16[768,512]{1,0:T(8,128)(2,1)S(1)}, bf16[768,512]{1,0:T(8,128)(2,1)S(1)}, u32[]{:S(2)}, u32[]{:S(2)}) collective-permute-start(bf16[768,512]{1,0:T(8,128)(2,1)S(1)} %bitcast.49), channel_id=1, source_target_pairs={{0,24},{8,0},{16,8},{24,16},{1,25},{9,1},{17,9},{25,17},{2,26},{10... | collective-permute-start | bytes 2359304 | tf_op jit(solution)/shard_map/ppermute | solution.py:235
  73.2 0.8 maximum_bitcast_fusion
  74.0 8.0 %all-to-all-start = ((bf16[8,32,640]{2,1,0:T(8,128)(2,1)}), bf16[8,32,640]{2,1,0:T(8,128)(2,1)S(1)}, u32[]{:S(2)}, u32[]{:S(2)}) async-start(bf16[8,32,640]{2,1,0:T(8,128)(2,1)} %maximum_bitcast_fusion), calls=%async_computation | async-start | bytes 655360 | tf_op jit(solution)/shard_map/all_to_all | solution.py:277
  82.2 3.9 %collective-permute-done.2.rest_1_ = bf16[768,512]{1,0:T(8,128)(2,1)S(1)} collective-permute-done((bf16[768,512]{1,0:T(8,128)(2,1)S(1)}, bf16[768,512]{1,0:T(8,128)(2,1)S(1)}, u32[]{:S(2)}, u32[]{:S(2)}) %collective-permute-start.2) | collective-permute-done | bytes 786464 | tf_op jit(solution)/shard_map/ppermute | solution.py:234
  86.0 0.8 slice.37
  86.9 1.9 %collective-permute-start.4 = (bf16[384,512]{1,0:T(8,128)(2,1)}, bf16[384,512]{1,0:T(8,128)(2,1)S(1)}, u32[]{:S(2)}, u32[]{:S(2)}) collective-permute-start(bf16[384,512]{1,0:T(8,128)(2,1)} %slice.37), channel_id=1, source_target_pairs={{0,8},{8,16},{16,24},{24,0},{1,9},{9,17},{17,25},{25,1},{2,10},{10... | collective-permute-start | bytes 1179656 | tf_op jit(solution)/shard_map/ppermute | solution.py:236
  88.8 0.9 slice.38
  89.7 4.6 %collective-permute-start.5 = (bf16[384,512]{1,0:T(8,128)(2,1)}, bf16[384,512]{1,0:T(8,128)(2,1)S(1)}, u32[]{:S(2)}, u32[]{:S(2)}) collective-permute-start(bf16[384,512]{1,0:T(8,128)(2,1)} %slice.38), channel_id=1, source_target_pairs={{0,24},{8,0},{16,8},{24,16},{1,25},{9,1},{17,9},{25,17},{2,26},{10... | collective-permute-start | bytes 1179656 | tf_op jit(solution)/shard_map/ppermute | solution.py:237
  94.3 1.2 slice.26
  96.1 3.1 %fusion = (f32[1024,128]{1,0:T(8,128)}, f32[1024,128]{1,0:T(8,128)}) fusion(f32[128]{0:T(128)S(1)} %get-tuple-element.19, f32[128]{0:T(128)S(1)} %get-tuple-element.20, f32[1024]{0:T(1024)S(1)} %add_convert_fusion), kind=kLoop, calls=%fused_computation.3 | loop fusion | flops 262144 | bytes 1053696 | tf_op jit(solution)/shard_map/mul | solution.py:315
  99.3 0.7 copy-done.5
  100.1 9.1 %project.1 = bf16[4,1024,128]{2,1,0:T(8,128)(2,1)} custom-call(s32[1]{0:T(128)} %bitcast.5.core_ref, bf16[512,3072]{1,0:T(8,128)(2,1)} %reorder_hidden.1.own_ref, bf16[512,3072]{1,0:T(8,128)(2,1)} %collective-permute-done.other_ref, bf16[768,512]{1,0:T(8,128)(2,1)} %bitcast.50, bf16[768,512]{1,0:T(8,128)(2,1)} %copy-done.3, bf16[768,512]{1,0:T(8,128)(2,1)} %copy-done.4, ...), custom_call_target="tpu_custom_call" | custom-call | tf_op jit(solution)/shard_map/project/pallas_call | solution.py:100
  109.2 5.8 %all-to-all-start.2 = ((bf16[4,1024,128]{2,1,0:T(8,128)(2,1)}), bf16[4,1024,128]{2,1,0:T(8,128)(2,1)S(1)}, u32[]{:S(2)}, u32[]{:S(2)}) async-start(bf16[4,1024,128]{2,1,0:T(8,128)(2,1)} %project.1), calls=%async_computation.2 | async-start | bytes 2097152 | tf_op jit(solution)/shard_map/all_to_all | solution.py:318
  115.0 0.7 slice.36.query_ref
  116.3 2.1 %tile.19.last_ref = s32[8,256,1]{2,1,0:T(8,128)} reshape(s32[8,8,32]{2,1,0:T(8,128)S(1)} %tile.17) | data formatting | bytes 16384 | tf_op jit(solution)/shard_map/tile | solution.py:304
  118.4 0.8 fusion.4
  119.2 1.3 fusion.5
  120.4 2.5 %prepare_queries.1.query_ref = bf16[8,256,128]{2,1,0:T(8,128)(2,1)} custom-call(bf16[256,512]{1,0:T(8,128)(2,1)} %slice.36.query_ref, bf16[256,256]{1,0:T(8,128)(2,1)} %get-tuple-element.12.pick_ref, f32[256,128]{1,0:T(8,128)} %get-tuple-element.10.cos_ref, f32[256,128]{1,0:T(8,128)} %get-tuple-element.9.sin_ref), custom_call_target="tpu_custom_call" | custom-call | tf_op jit(solution)/shard_map/prepare_queries/pallas_call | solution.py:132
  123.7 15.6 %all-to-all-done.2 = bf16[4,1024,128]{2,1,0:T(8,128)(2,1)S(1)} async-done(((bf16[4,1024,128]{2,1,0:T(8,128)(2,1)}), bf16[4,1024,128]{2,1,0:T(8,128)(2,1)S(1)}, u32[]{:S(2)}, u32[]{:S(2)}) %all-to-all-start.2) | async-done | bytes 1048608 | tf_op jit(solution)/shard_map/all_to_all | solution.py:318
  139.3 1.0 copy-done.1
  140.3 24.4 %attend.1 = bf16[256,512]{1,0:T(8,128)(2,1)} custom-call(s32[2,8]{1,0:T(2,128)} %pad_add_fusion.bound_ref, bf16[8,256,128]{2,1,0:T(8,128)(2,1)} %prepare_queries.1.query_ref, bf16[4096,128]{1,0:T(8,128)(2,1)} %bitcast.47, s32[8,256,1]{2,1,0:T(8,128)} %tile.19.last_ref, bf16[256,256]{1,0:T(8,128)(2,1)} %get-tuple-element.11.unpick_ref), custom_call_target="tpu_custom_call" | custom-call | tf_op jit(solution)/shard_map/attend/pallas_call | solution.py:208
  164.6 14.4 %all_to_all.21 = bf16[8,32,512]{2,1,0:T(8,128)(2,1)S(1)} all-to-all(bf16[8,32,512]{2,1,0:T(8,128)(2,1)} %bitcast.55), channel_id=1, replica_groups=mesh['yh'=2,'z'=8,'x'=4,'yl'=4,'co'=2] {'yl','co'}, dimensions={0} | all-to-all | bytes 524288 | tf_op jit(solution)/shard_map/all_to_all | solution.py:321
  179.2 0.8 reshape.465
  (63 shorter events, 3.3 us)
Async XLA Ops:
  0.0 0.7 copy-start
  6.8 23.6 %copy-start.8 = (bf16[45,1024]{1,0:T(8,128)(2,1)S(1)}, bf16[45,1024]{1,0:T(8,128)(2,1)}, u32[]{:S(2)}) copy-start(bf16[45,1024]{1,0:T(8,128)(2,1)} %param.8) | copy-start | bytes 276484
  21.5 51.4 %copy-start.7 = (bf16[1,32,4096]{2,1,0:T(8,128)(2,1)S(1)}, bf16[1,32,4096]{2,1,0:T(8,128)(2,1)}, u32[]{:S(2)}) copy-start(bf16[1,32,4096]{2,1,0:T(8,128)(2,1)} %param.10) | copy-start | bytes 786436
  21.5 51.6 %copy-start.10 = (s32[1,32]{1,0:T(1,128)S(1)}, s32[1,32]{1,0:T(1,128)}, u32[]{:S(2)}) copy-start(s32[1,32]{1,0:T(1,128)} %param.12) | copy-start | bytes 388
  21.5 77.8 %collective-permute-start = (bf16[512,3072]{1,0:T(8,128)(2,1)}, bf16[512,3072]{1,0:T(8,128)(2,1)}, u32[]{:S(2)}, u32[]{:S(2)}) collective-permute-start(bf16[512,3072]{1,0:T(8,128)(2,1)} %reorder_hidden.1.own_ref), channel_id=1, source_target_pairs={{0,1},{1,0},{2,3},{3,2},{4,5},{5,4},{6,7},{7,6},{8,9},{9,8},{10,11... | collective-permute-start | bytes 9437192 | tf_op jit(solution)/shard_map/ppermute | solution.py:281
  30.8 9.1 %collective-permute-start.1 = (bf16[48,512]{1,0:T(8,128)(2,1)S(1)}, bf16[48,512]{1,0:T(8,128)(2,1)S(1)}, u32[]{:S(2)}, u32[]{:S(2)}) collective-permute-start(bf16[48,512]{1,0:T(8,128)(2,1)S(1)} %pad.4), channel_id=1, source_target_pairs={{0,256},{256,0},{1,257},{257,1},{2,258},{258,2},{3,259},{259,3},{4... | collective-permute-start | bytes 147464 | tf_op jit(solution)/shard_map/ppermute | solution.py:227
  39.9 54.4 %copy-start.9 = (f32[128]{0:T(128)S(1)}, f32[128]{0:T(128)}, u32[]{:S(2)}) copy-start(f32[128]{0:T(128)} %constant.95.clone) | copy-start | bytes 1540
  66.4 32.9 %copy-start.2 = (bf16[8,96,512]{2,1,0:T(8,128)(2,1)}, bf16[8,96,512]{2,1,0:T(8,128)(2,1)S(1)}, u32[]{:S(2)}) copy-start(bf16[8,96,512]{2,1,0:T(8,128)(2,1)S(1)} %all_to_all.20) | copy-start | bytes 2359300
  66.4 19.7 %collective-permute-start.2 = (bf16[768,512]{1,0:T(8,128)(2,1)S(1)}, bf16[768,512]{1,0:T(8,128)(2,1)S(1)}, u32[]{:S(2)}, u32[]{:S(2)}) collective-permute-start(bf16[768,512]{1,0:T(8,128)(2,1)S(1)} %bitcast.48), channel_id=1, source_target_pairs={{0,8},{8,16},{16,24},{24,0},{1,9},{9,17},{17,25},{25,1},{2,10},{10... | collective-permute-start | bytes 2359304 | tf_op jit(solution)/shard_map/ppermute | solution.py:234
  69.5 19.3 %collective-permute-start.3 = (bf16[768,512]{1,0:T(8,128)(2,1)S(1)}, bf16[768,512]{1,0:T(8,128)(2,1)S(1)}, u32[]{:S(2)}, u32[]{:S(2)}) collective-permute-start(bf16[768,512]{1,0:T(8,128)(2,1)S(1)} %bitcast.49), channel_id=1, source_target_pairs={{0,24},{8,0},{16,8},{24,16},{1,25},{9,1},{17,9},{25,17},{2,26},{10... | collective-permute-start | bytes 2359304 | tf_op jit(solution)/shard_map/ppermute | solution.py:235
  74.0 35.2 %all-to-all-start = ((bf16[8,32,640]{2,1,0:T(8,128)(2,1)}), bf16[8,32,640]{2,1,0:T(8,128)(2,1)S(1)}, u32[]{:S(2)}, u32[]{:S(2)}) async-start(bf16[8,32,640]{2,1,0:T(8,128)(2,1)} %maximum_bitcast_fusion), calls=%async_computation | async-start | bytes 655360 | tf_op jit(solution)/shard_map/all_to_all | solution.py:277
  86.0 13.2 %copy-start.3 = (bf16[768,512]{1,0:T(8,128)(2,1)}, bf16[768,512]{1,0:T(8,128)(2,1)S(1)}, u32[]{:S(2)}) copy-start(bf16[768,512]{1,0:T(8,128)(2,1)S(1)} %collective-permute-done.2.rest_1_) | copy-start | bytes 2359300
  86.9 12.3 %collective-permute-start.4 = (bf16[384,512]{1,0:T(8,128)(2,1)}, bf16[384,512]{1,0:T(8,128)(2,1)S(1)}, u32[]{:S(2)}, u32[]{:S(2)}) collective-permute-start(bf16[384,512]{1,0:T(8,128)(2,1)} %slice.37), channel_id=1, source_target_pairs={{0,8},{8,16},{16,24},{24,0},{1,9},{9,17},{17,25},{25,1},{2,10},{10... | collective-permute-start | bytes 1179656 | tf_op jit(solution)/shard_map/ppermute | solution.py:236
  88.8 10.5 %copy-start.4 = (bf16[768,512]{1,0:T(8,128)(2,1)}, bf16[768,512]{1,0:T(8,128)(2,1)S(1)}, u32[]{:S(2)}) copy-start(bf16[768,512]{1,0:T(8,128)(2,1)S(1)} %collective-permute-done.3.rest_2_) | copy-start | bytes 2359300
  89.7 9.6 %collective-permute-start.5 = (bf16[384,512]{1,0:T(8,128)(2,1)}, bf16[384,512]{1,0:T(8,128)(2,1)S(1)}, u32[]{:S(2)}, u32[]{:S(2)}) collective-permute-start(bf16[384,512]{1,0:T(8,128)(2,1)} %slice.38), channel_id=1, source_target_pairs={{0,24},{8,0},{16,8},{24,16},{1,25},{9,1},{17,9},{25,17},{2,26},{10... | collective-permute-start | bytes 1179656 | tf_op jit(solution)/shard_map/ppermute | solution.py:237
  99.2 0.8 copy-start.5
  99.3 0.8 copy-start.6
  109.2 30.0 %all-to-all-start.2 = ((bf16[4,1024,128]{2,1,0:T(8,128)(2,1)}), bf16[4,1024,128]{2,1,0:T(8,128)(2,1)S(1)}, u32[]{:S(2)}, u32[]{:S(2)}) async-start(bf16[4,1024,128]{2,1,0:T(8,128)(2,1)} %project.1), calls=%async_computation.2 | async-start | bytes 2097152 | tf_op jit(solution)/shard_map/all_to_all | solution.py:318
  139.3 1.0 copy-start.1

commit v2 on v1

--- a/solution.py
+++ b/solution.py
@@ -8,15 +8,17 @@
 from jax.experimental.pallas import tpu as pltpu
 from jax.sharding import Mesh, PartitionSpec as P
 
+
 HEADS = 64
 KV_HEADS = 8
 WIDTH = 64
 GROUP = HEADS // KV_HEADS
 LANES = 2 * WIDTH
 ROPE_BASE = 150000.0
+LOG2_E = 1.4426950408889634
 PAD_ROWS = 48
 QUERY_BLOCK = 32
-KEY_BLOCK = 512
+KEY_BLOCK = 1024
 ROLL = ("yh", "z", "x")
 SEQ = ("yl", "co")
 
@@ -66,44 +68,76 @@
     )
 
 
-def project_kernel(core_ref, own_ref, other_ref, *rest):
-    pieces, (cos_ref, sin_ref, out_ref) = rest[:-3], rest[-3:]
+def product(hidden_ref, pieces):
+    total, offset = None, 0
+    for piece in pieces:
+        size = piece.shape[0]
+        part = jnp.dot(
+            hidden_ref[:, offset : offset + size],
+            piece[...],
+            preferred_element_type=jnp.float32,
+        )
+        total = part if total is None else total + part
+        offset += size
+    return total
+
+
+def first_half_kernel(core_ref, own_ref, other_ref, *rest):
+    pieces, out_ref = rest[:-1], rest[-1]
+    rows = own_ref.shape[0]
+    core = core_ref[0]
+    for hidden_ref, place in ((own_ref, core), (other_ref, 1 - core)):
+        out_ref[pl.ds(pl.multiple_of(place * rows, rows), rows), :] = product(
+            hidden_ref, pieces
+        )
+
+
+def first_half(core, own, other, pieces):
+    vmem = pl.BlockSpec(memory_space=pltpu.VMEM)
+    depth = sum(piece.shape[0] for piece in pieces)
+    part = pl.BlockSpec((own.shape[0], depth), lambda i: (0, 0))
+    return pl.pallas_call(
+        first_half_kernel,
+        grid=(1,),
+        in_specs=[pl.BlockSpec(memory_space=pltpu.SMEM), part, part] + [vmem] * len(pieces),
+        out_specs=vmem,
+        out_shape=jax.ShapeDtypeStruct((2 * own.shape[0], pieces[0].shape[1]), jnp.float32),
+        name="first_half",
+    )(core, own, other, *pieces)
+
+
+def project_kernel(core_ref, own_ref, other_ref, total_ref, cos_ref, sin_ref, *rest):
+    pieces, out_ref = rest[:-1], rest[-1]
     rows = own_ref.shape[0]
     core = core_ref[0]
     lane = lax.broadcasted_iota(jnp.int32, (rows, LANES), 1)
     for hidden_ref, place in ((own_ref, core), (other_ref, 1 - core)):
-        total = None
-        offset = 0
-        for piece in pieces:
-            size = piece.shape[0]
-            part = jnp.dot(
-                hidden_ref[:, offset : offset + size],
-                piece[...],
-                preferred_element_type=jnp.float32,
-            )
-            total = part if total is None else total + part
-            offset += size
-        base = pl.multiple_of(place * rows, rows)
-        cosine = cos_ref[pl.ds(base, rows), :]
-        sine = sin_ref[pl.ds(base, rows), :]
+        here = pl.ds(pl.multiple_of(place * rows, rows), rows)
+        total = total_ref[here, :] + product(hidden_ref, pieces)
+        cosine = cos_ref[here, :]
+        sine = sin_ref[here, :]
         for head in range(out_ref.shape[0]):
             x = total[:, head * LANES : (head + 1) * LANES]
-            out_ref[head, pl.ds(base, rows), :] = (
-                x * cosine + swap_halves(x, lane) * sine
-            ).astype(jnp.bfloat16)
-
-
-def project(core, own, other, pieces, cosine, sine):
+            out_ref[head, here, :] = (x * cosine + swap_halves(x, lane) * sine).astype(
+                jnp.bfloat16
+            )
+
+
+def project(core, own, other, pieces, total, cosine, sine):
     rows = own.shape[0]
-    heads = pieces[0].shape[1] // LANES
+    heads = total.shape[1] // LANES
     vmem = pl.BlockSpec(memory_space=pltpu.VMEM)
+    depth = sum(piece.shape[0] for piece in pieces)
+    part = pl.BlockSpec((rows, depth), lambda i: (0, own.shape[1] // depth - 1))
     return pl.pallas_call(
         project_kernel,
-        in_specs=[pl.BlockSpec(memory_space=pltpu.SMEM)] + [vmem] * (len(pieces) + 4),
+        grid=(1,),
+        in_specs=[pl.BlockSpec(memory_space=pltpu.SMEM), part, part]
+        + [vmem] * (3 + len(pieces)),
         out_specs=vmem,
         out_shape=jax.ShapeDtypeStruct((heads, 2 * rows, LANES), jnp.bfloat16),
         name="project",
-    )(core, own, other, *pieces, cosine, sine)
+    )(core, own, other, total, cosine, sine, *pieces)
 
 
 def prepare_kernel(query_ref, pick_ref, cos_ref, sin_ref, out_ref):
@@ -141,7 +175,7 @@
 
 
 def attend_kernel(
-    bound_ref, query_ref, kv_ref, last_ref, unpick_ref, out_ref, value_ref, sorted_ref
+    bound_ref, query_ref, kv_ref, last_ref, unpick_ref, out_ref, value_ref, score_ref, sorted_ref
 ):
     blocks = query_ref.shape[0]
     rows = query_ref.shape[1]
@@ -149,50 +183,54 @@
     lane_kv = lax.broadcasted_iota(jnp.int32, (KEY_BLOCK, LANES), 1)
     for step in range(keys // KEY_BLOCK):
         here = slice(step * KEY_BLOCK, (step + 1) * KEY_BLOCK)
-        value_ref[here, :] = jnp.where(
-            lane_kv < WIDTH, jnp.ones((), jnp.bfloat16), kv_ref[here, :]
-        )
-    column = lax.broadcasted_iota(jnp.int32, (rows, KEY_BLOCK), 1)
+        value_ref[:, here] = jnp.where(
+            lane_kv < WIDTH, 1.0, kv_ref[here, :].astype(jnp.float32)
+        ).T.astype(jnp.bfloat16)
+    key_index = lax.broadcasted_iota(jnp.int32, (KEY_BLOCK, rows), 0)
     lane = lax.broadcasted_iota(jnp.int32, (QUERY_BLOCK, LANES), 1)
 
     def one_block(block, carry):
         query = query_ref[block]
         last = last_ref[block]
-
-        def step(masked, index, state):
-            top, total = state
+        full, count = bound_ref[0, block], bound_ref[1, block]
+
+        def score(masked, index, top):
             base = pl.multiple_of(index * KEY_BLOCK, KEY_BLOCK)
             scores = lax.dot_general(
+                kv_ref[pl.ds(base, KEY_BLOCK), :],
                 query,
-                kv_ref[pl.ds(base, KEY_BLOCK), :],
                 (((1,), (1,)), ((), ())),
                 preferred_element_type=jnp.float32,
             )
+            scores = scores * LOG2_E
             if masked:
-                scores = jnp.where(column <= last - base, scores, -1e30)
-            new_top = jnp.maximum(top, jnp.max(scores, axis=1, keepdims=True))
-            expo = jnp.exp(scores - new_top)
-            part = jnp.dot(
+                scores = jnp.where(key_index <= last - base, scores, -1e30)
+            score_ref[pl.ds(base, KEY_BLOCK), :] = scores
+            return jnp.maximum(top, jnp.max(scores.reshape(-1, 8, rows), axis=0))
+
+        top = jnp.full((8, rows), -1e30, jnp.float32)
+        top = lax.fori_loop(0, full, functools.partial(score, False), top)
+        top = lax.fori_loop(full, count, functools.partial(score, True), top)
+        top = jnp.max(top, axis=0, keepdims=True)
+
+        def weigh(index, total):
+            base = pl.multiple_of(index * KEY_BLOCK, KEY_BLOCK)
+            expo = jnp.exp2(score_ref[pl.ds(base, KEY_BLOCK), :] - top)
+            return total + jnp.dot(
+                value_ref[:, pl.ds(base, KEY_BLOCK)],
                 expo.astype(jnp.bfloat16),
-                value_ref[pl.ds(base, KEY_BLOCK), :],
                 preferred_element_type=jnp.float32,
             )
-            return new_top, total * jnp.exp(top - new_top) + part
-
-        state = (
-            jnp.full((rows, 1), -1e30, jnp.float32),
-            jnp.zeros((rows, LANES), jnp.float32),
-        )
-        full = bound_ref[0, block]
-        state = lax.fori_loop(0, full, functools.partial(step, False), state)
-        _, total = lax.fori_loop(full, bound_ref[1, block], functools.partial(step, True), state)
-        result = total / pltpu.roll(total, WIDTH, 1)
+
+        total = lax.fori_loop(0, count, weigh, jnp.zeros((LANES, rows), jnp.float32))
+        result = total[WIDTH:] / total[:WIDTH]
+        result = jnp.concatenate([result, result], 0).T
         place = pl.multiple_of(block * QUERY_BLOCK, QUERY_BLOCK)
         for pair in range(GROUP // 2):
             even = result[2 * pair * QUERY_BLOCK : (2 * pair + 1) * QUERY_BLOCK]
             odd = result[(2 * pair + 1) * QUERY_BLOCK : (2 * pair + 2) * QUERY_BLOCK]
             sorted_ref[pl.ds(place, QUERY_BLOCK), pair * LANES : (pair + 1) * LANES] = jnp.where(
-                lane < WIDTH, pltpu.roll(even, WIDTH, 1), odd
+                lane < WIDTH, even, odd
             ).astype(jnp.bfloat16)
         return carry
 
@@ -205,17 +243,26 @@
 def attend(bounds, query, kv, last, unpick):
     vmem = pl.BlockSpec(memory_space=pltpu.VMEM)
     count = unpick.shape[0]
+    keys = kv.shape[0]
     return pl.pallas_call(
         attend_kernel,
         in_specs=[pl.BlockSpec(memory_space=pltpu.SMEM)] + [vmem] * 4,
         out_specs=vmem,
         out_shape=jax.ShapeDtypeStruct((count, GROUP * WIDTH), jnp.bfloat16),
         scratch_shapes=[
-            pltpu.VMEM(kv.shape, jnp.bfloat16),
+            pltpu.VMEM((LANES, keys), jnp.bfloat16),
+            pltpu.VMEM((keys, query.shape[1]), jnp.float32),
             pltpu.VMEM((count, GROUP * WIDTH), jnp.bfloat16),
         ],
         name="attend",
     )(bounds, query, kv, last, unpick)
+
+
+def spread(x, axis):
+    size = lax.axis_size(axis)
+    copies = jnp.broadcast_to(x[None], (size,) + x.shape)
+    whole = lax.all_to_all(copies, axis, 0, 0, tiled=True)
+    return whole.reshape((-1,) + x.shape[1:])
 
 
 def gather_weight(blocks):
@@ -224,31 +271,24 @@
     split = blocks.reshape(block_rows, KV_HEADS // 2, 2, LANES)
     mine = lax.dynamic_index_in_dim(split, core, 2, False).reshape(block_rows, -1)
     mine = jnp.pad(mine, ((0, PAD_ROWS - block_rows), (0, 0)))
-    far = lax.ppermute(mine, "yh", ring(2, 1))
-    both = jnp.concatenate([mine, far], 0)
-    plane = lax.all_to_all(
-        jnp.broadcast_to(both[None], (8,) + both.shape), "z", 0, 0, tiled=True
-    )
-    plane = plane.reshape(8 * 2 * PAD_ROWS, -1)
+    plane = spread(mine, ("yh", "z"))
     half = plane.shape[0] // 2
-    below = lax.ppermute(plane, "x", ring(4, 1))
-    above = lax.ppermute(plane, "x", ring(4, -1))
-    across_low = lax.ppermute(below[:half], "x", ring(4, 1))
-    across_high = lax.ppermute(above[half:], "x", ring(4, -1))
-    return plane, below, above, across_low, across_high
+    up, down = ring(4, 1), ring(4, -1)
+    below = lax.ppermute(plane, "x", up)
+    above = lax.ppermute(plane, "x", down)
+    low = lax.ppermute(below[:half], "x", up)
+    high = lax.ppermute(above[half:], "x", down)
+    return (plane, below, above), (low, high)
 
 
 def slot_order(block_of):
-    yh, z, x = (lax.axis_index(a) for a in ROLL)
+    x = lax.axis_index("x")
     xs = jnp.stack([x, x + 3, x + 1, x + 2]) % 4
-    ys = jnp.stack([yh, 1 - yh])
-    stored = (
-        ys[None, None, :] * 32 + jnp.arange(8)[None, :, None] * 4 + xs[:, None, None]
-    ).reshape(-1)
-    return block_of[stored]
-
-
-def shards(hidden, blocks, block_of, queries, key_pos, query_pos):
+    stored = jnp.arange(16)[None, :] * 4 + xs[:, None]
+    return block_of[stored.reshape(-1)]
+
+
+def attention(hidden, blocks, block_of, queries, key_pos, query_pos):
     core = lax.axis_index("co")
     seq_index = lax.axis_index(SEQ)
     seq = lax.axis_size(SEQ)
@@ -276,7 +316,7 @@
     payload = jnp.concatenate([queries[0].reshape(query_rows, KV_HEADS, GROUP * WIDTH), extra], -1)
     payload = lax.all_to_all(payload.transpose(1, 0, 2), SEQ, 0, 0, tiled=True)
 
-    pieces = gather_weight(blocks)
+    near, far = gather_weight(blocks)
     own = reorder(hidden[0], source)
     other = lax.ppermute(own, "co", ring(2, 1))
 
@@ -298,10 +338,8 @@
     unpick = (rank[:, None] == order[None, :]).astype(jnp.bfloat16)
     last = sorted_pos - start
     by_block = last.reshape(-1, QUERY_BLOCK)
-    bounds = jnp.stack(
-        [(by_block[:, 0] + 1) // KEY_BLOCK, by_block[:, -1] // KEY_BLOCK + 1]
-    )
-    last_rows = jnp.tile(by_block, (1, GROUP))[..., None]
+    bounds = jnp.stack([(by_block[:, 0] + 1) // KEY_BLOCK, by_block[:, -1] // KEY_BLOCK + 1])
+    last_rows = jnp.tile(by_block, (1, GROUP))[:, None, :]
 
     sign = jnp.asarray(np.where(np.arange(LANES) % WIDTH < WIDTH // 2, -1.0, 1.0), jnp.float32)
     freq = lane_frequencies(LANES)
@@ -314,7 +352,9 @@
     key_angle = chip_pos.astype(jnp.float32)[:, None] * jnp.where(is_key, freq, 0.0)[None, :]
     key_sine = jnp.sin(key_angle) * jnp.where(is_key, sign, 0.0)
 
-    kv = project(core.reshape(1), own, other, pieces, jnp.cos(key_angle), key_sine)
+    place = core.reshape(1)
+    total = first_half(place, own, other, near)
+    kv = project(place, own, other, far, total, jnp.cos(key_angle), key_sine)
     kv = lax.all_to_all(kv, "yl", 0, 0, tiled=True).reshape(keys, LANES)
     context = attend(bounds, prepared, kv, last_rows, unpick)
     context = context.reshape(seq, query_rows, GROUP * WIDTH)
@@ -325,7 +365,7 @@
 def solution(mesh):
     fine = Mesh(mesh.devices.reshape(2, 8, 4, 4, 2), ROLL + SEQ)
     return jax.shard_map(
-        shards,
+        attention,
         mesh=fine,
         in_specs=(
             P(ROLL, SEQ, None),

time: 182 us -> 179 us (0.984)
  waiting for transfers between devices: 26.5 us -> 21.4 us
  Pallas kernels: 50.7 us -> 46.9 us
  blocking collectives: 40.8 us -> 44.5 us
  local copies, waits for them, and re-layouts: 15.7 us -> 18.2 us
    ppermute x6 -> x5, waiting for transfers between devices: 10.9 us -> 3.47 us  [the longest x1 3.46 us: gather_weight(): below = lax.ppermute(plane, 'x', up)]
    pallas_call x1, Pallas kernels: 24.4 us -> 17.3 us  [attend(): pl.pallas_call(attend_kernel, in_specs=[pl.BlockSpec(memory_space=pltpu.S...]
    all_to_all x2, blocking collectives: 40.8 us -> 44.5 us  [the longest x1 31 us: spread(): whole = lax.all_to_all(copies, axis, 0, 0, tiled=True)]
    pallas_call x1 -> x2, Pallas kernels: 9.12 us -> 12.5 us  [the longest x1 7.12 us: first_half(): pl.pallas_call(first_half_kernel, grid=(1,), in_specs=[pl.BlockSpec(memor...]
    all_to_all x2, starting transfers between devices: 13.8 us -> 16.8 us  [the longest x1 9.63 us: attention(): payload = lax.all_to_all(payload.transpose(1, 0, 2), SEQ, 0, 0, tiled=True)]
    all_to_all x2, waiting for transfers between devices: 15.6 us -> 18 us  [the longest x1 18 us: attention(): kv = lax.all_to_all(kv, 'yl', 0, 0, tiled=True).reshape(keys, LANES)]
    ppermute x6 -> x5, starting transfers between devices: 23.9 us -> 21.8 us  [the longest x1 8.87 us: attention(): other = lax.ppermute(own, 'co', ring(2, 1))]
    slice x4, local copies, waits for them, and re-layouts: 3.59 us -> 5.49 us  [the longest x1 1.82 us: gather_weight(): high = lax.ppermute(above[half:], 'x', down)]
  transfers between devices with their start and end apart: 8 -> 7, of which waited for: 4 -> 2; matrix products, arithmetic and copies ran while one was open for 8% -> 9% of each run, Pallas kernels for 6% -> 8%
where the time goes in v2:
time: 179 us; the launch traced here: 178 us
  Pallas kernels  46.9 us (26%)
  blocking collectives  44.5 us (25%)
  starting transfers between devices  38.6 us (22%)
  waiting for transfers between devices  21.4 us (12%)
  local copies, waits for them, and re-layouts  18.2 us (10%)
  other arithmetic  7.46 us (4%)
    all_to_all x1, blocking collectives, spread(): whole = lax.all_to_all(copies, axis, 0, 0, tiled=True)  31 us
    all_to_all x1, waiting for transfers between devices, attention(): kv = lax.all_to_all(kv, 'yl', 0, 0, tiled=True).reshape(keys, LANES)  18 us
    pallas_call x1, Pallas kernels, attend(): pl.pallas_call(attend_kernel, in_specs=[pl.BlockSpec(memory_space=pltpu.S...  17.3 us
    pallas_call x1, Pallas kernels, reorder(): pl.pallas_call(reorder_kernel, grid=(columns // tile,), in_specs=[pl.Bloc...  14.6 us
    all_to_all x1, blocking collectives, attention(): context = lax.all_to_all(context, SEQ, 0, 0, tiled=True)  13.6 us
    all_to_all x1, starting transfers between devices, attention(): payload = lax.all_to_all(payload.transpose(1, 0, 2), SEQ, 0, 0, tiled=True)  9.63 us
    ppermute x1, starting transfers between devices, attention(): other = lax.ppermute(own, 'co', ring(2, 1))  8.87 us
    unnamed x16, local copies, waits for them, and re-layouts  7.77 us
  transfers between devices with their start and end apart: 7, of which 2 were waited for; matrix products, arithmetic and copies ran while one was open for 9% of the time, Pallas kernels for 8%

profile of v2, /device:TPU:1, one launch (start us, length us, event | category | flops | bytes accessed | tf_op | source)
XLA Modules:
  0.0 178.1 jit_solution(7450571210602808003)
XLA Ops:
  0.7 0.8 gather_fusion
  1.5 0.7 select_n.83.source_ref
  2.2 4.6 %copy.21 = bf16[1,512,2880]{2,1,0:T(8,128)(2,1)} copy(bf16[1,512,2880]{1,2,0:T(8,128)(2,1)} %param.7) | data formatting | bytes 5898240 | tf_op args[0]
  6.8 14.6 %reorder_hidden.1.own_ref = bf16[512,3072]{1,0:T(8,128)(2,1)} custom-call(s32[1,3072]{1,0:T(1,128)} %select_n.83.source_ref, bf16[512,2880]{1,0:T(8,128)(2,1)} %bitcast.44), custom_call_target="tpu_custom_call" | custom-call | tf_op jit(solution)/shard_map/reorder_hidden/pallas_call | solution.py:49
  21.5 8.9 %collective-permute-start = (bf16[512,3072]{1,0:T(8,128)(2,1)}, bf16[512,3072]{1,0:T(8,128)(2,1)S(1)}, u32[]{:S(2)}, u32[]{:S(2)}) collective-permute-start(bf16[512,3072]{1,0:T(8,128)(2,1)} %reorder_hidden.1.own_ref), channel_id=1, source_target_pairs={{0,1},{1,0},{2,3},{3,2},{4,5},{5,4},{6,7},{7,6},{8,9},{9,8},{10,11... | collective-permute-start | bytes 9437192 | tf_op jit(solution)/shard_map/ppermute | solution.py:321
  30.4 0.9 reshape.410
  31.8 31.0 %all_to_all.20 = bf16[16,48,512]{2,1,0:T(8,128)(2,1)} all-to-all(bf16[16,48,512]{2,1,0:T(8,128)(2,1)S(1)} %broadcast_in_dim.33), channel_id=1, replica_groups=mesh['yh'=2,'z'=8,'x'=4,'yl'=4,'co'=2] {'yh','z'}, dimensions={0} | all-to-all | bytes 1572864 | tf_op jit(solution)/shard_map/all_to_all | solution.py:264
  62.8 3.1 %collective-permute-start.1 = (bf16[768,512]{1,0:T(8,128)(2,1)}, bf16[768,512]{1,0:T(8,128)(2,1)}, u32[]{:S(2)}, u32[]{:S(2)}) collective-permute-start(bf16[768,512]{1,0:T(8,128)(2,1)} %bitcast.12.rest_0_), channel_id=1, source_target_pairs={{0,8},{8,16},{16,24},{24,0},{1,9},{9,17},{17,25},{25,1},{2,10},{10... | collective-permute-start | bytes 2359304 | tf_op jit(solution)/shard_map/ppermute | solution.py:277
  65.9 3.4 %collective-permute-start.2 = (bf16[768,512]{1,0:T(8,128)(2,1)}, bf16[768,512]{1,0:T(8,128)(2,1)}, u32[]{:S(2)}, u32[]{:S(2)}) collective-permute-start(bf16[768,512]{1,0:T(8,128)(2,1)} %bitcast.12.rest_0_), channel_id=1, source_target_pairs={{0,24},{8,0},{16,8},{24,16},{1,25},{9,1},{17,9},{25,17},{2,26},{10... | collective-permute-start | bytes 2359304 | tf_op jit(solution)/shard_map/ppermute | solution.py:278
  69.6 0.8 maximum_bitcast_fusion
  70.5 9.6 %all-to-all-start = ((bf16[8,32,640]{2,1,0:T(8,128)(2,1)}), bf16[8,32,640]{2,1,0:T(8,128)(2,1)S(1)}, u32[]{:S(2)}, u32[]{:S(2)}) async-start(bf16[8,32,640]{2,1,0:T(8,128)(2,1)} %maximum_bitcast_fusion), calls=%async_computation | async-start | bytes 655360 | tf_op jit(solution)/shard_map/all_to_all | solution.py:317
  80.2 3.5 %collective-permute-done.1.rest_1_ = bf16[768,512]{1,0:T(8,128)(2,1)} collective-permute-done((bf16[768,512]{1,0:T(8,128)(2,1)}, bf16[768,512]{1,0:T(8,128)(2,1)}, u32[]{:S(2)}, u32[]{:S(2)}) %collective-permute-start.1) | collective-permute-done | bytes 786464 | tf_op jit(solution)/shard_map/ppermute | solution.py:277
  83.6 1.8 %slice.37 = bf16[384,512]{1,0:T(8,128)(2,1)} slice(bf16[768,512]{1,0:T(8,128)(2,1)} %collective-permute-done.1.rest_1_), slice={[0:384], [0:512]} | slice | bytes 786432 | tf_op jit(solution)/shard_map/slice | solution.py:279
  85.4 1.9 %collective-permute-start.3 = (bf16[384,512]{1,0:T(8,128)(2,1)}, bf16[384,512]{1,0:T(8,128)(2,1)}, u32[]{:S(2)}, u32[]{:S(2)}) collective-permute-start(bf16[384,512]{1,0:T(8,128)(2,1)} %slice.37), channel_id=1, source_target_pairs={{0,8},{8,16},{16,24},{24,0},{1,9},{9,17},{17,25},{25,1},{2,10},{10... | collective-permute-start | bytes 1179656 | tf_op jit(solution)/shard_map/ppermute | solution.py:279
  87.4 1.8 %slice.38 = bf16[384,512]{1,0:T(8,128)(2,1)} slice(bf16[768,512]{1,0:T(8,128)(2,1)} %collective-permute-done.2.rest_2_), slice={[384:768], [0:512]} | slice | bytes 786432 | tf_op jit(solution)/shard_map/slice | solution.py:280
  89.2 4.6 %collective-permute-start.4 = (bf16[384,512]{1,0:T(8,128)(2,1)}, bf16[384,512]{1,0:T(8,128)(2,1)}, u32[]{:S(2)}, u32[]{:S(2)}) collective-permute-start(bf16[384,512]{1,0:T(8,128)(2,1)} %slice.38), channel_id=1, source_target_pairs={{0,24},{8,0},{16,8},{24,16},{1,25},{9,1},{17,9},{25,17},{2,26},{10... | collective-permute-start | bytes 1179656 | tf_op jit(solution)/shard_map/ppermute | solution.py:280
  93.8 1.2 slice.26
  95.6 3.1 %fusion = (f32[1024,128]{1,0:T(8,128)}, f32[1024,128]{1,0:T(8,128)}) fusion(f32[128]{0:T(128)S(1)} %get-tuple-element.19, f32[128]{0:T(128)S(1)} %get-tuple-element.20, f32[1024]{0:T(1024)S(1)} %add_convert_fusion), kind=kLoop, calls=%fused_computation.3 | loop fusion | flops 262144 | bytes 1053696 | tf_op jit(solution)/shard_map/mul | solution.py:353
  98.7 1.7 copy-done.1
  100.4 7.1 %first_half.1.total_ref = f32[1024,512]{1,0:T(8,128)} custom-call(s32[1]{0:T(128)} %bitcast.5.core_ref, bf16[512,3072]{1,0:T(8,128)(2,1)} %reorder_hidden.1.own_ref, bf16[512,3072]{1,0:T(8,128)(2,1)} %copy-done.1, bf16[768,512]{1,0:T(8,128)(2,1)} %bitcast.12.rest_0_, bf16[768,512]{1,0:T(8,128)(2,1)} %collective-permute-done.1.rest_1_, ...), custom_call_target="tpu_custom_call" | custom-call | tf_op jit(solution)/shard_map/first_half/pallas_call | solution.py:99
  107.5 5.3 %project.1 = bf16[4,1024,128]{2,1,0:T(8,128)(2,1)} custom-call(s32[1]{0:T(128)} %bitcast.5.core_ref, bf16[512,3072]{1,0:T(8,128)(2,1)} %reorder_hidden.1.own_ref, bf16[512,3072]{1,0:T(8,128)(2,1)} %copy-done.1, f32[1024,512]{1,0:T(8,128)} %first_half.1.total_ref, f32[1024,128]{1,0:T(8,128)} %get-tuple-element.8.cos_ref, ...), custom_call_target="tpu_custom_call" | custom-call | tf_op jit(solution)/shard_map/project/pallas_call | solution.py:132
  112.8 7.2 %all-to-all-start.2 = ((bf16[4,1024,128]{2,1,0:T(8,128)(2,1)}), bf16[4,1024,128]{2,1,0:T(8,128)(2,1)S(1)}, u32[]{:S(2)}, u32[]{:S(2)}) async-start(bf16[4,1024,128]{2,1,0:T(8,128)(2,1)} %project.1), calls=%async_computation.2 | async-start | bytes 2097152 | tf_op jit(solution)/shard_map/all_to_all | solution.py:358
  120.0 0.7 slice.36.query_ref
  121.3 0.7 tile.18.last_ref
  122.0 0.8 fusion.4
  122.8 1.2 fusion.5
  124.0 2.5 %prepare_queries.1.query_ref = bf16[8,256,128]{2,1,0:T(8,128)(2,1)} custom-call(bf16[256,512]{1,0:T(8,128)(2,1)} %slice.36.query_ref, bf16[256,256]{1,0:T(8,128)(2,1)} %get-tuple-element.12.pick_ref, f32[256,128]{1,0:T(8,128)} %get-tuple-element.10.cos_ref, f32[256,128]{1,0:T(8,128)} %get-tuple-element.9.sin_ref), custom_call_target="tpu_custom_call" | custom-call | tf_op jit(solution)/shard_map/prepare_queries/pallas_call | solution.py:166
  127.3 18.0 %all-to-all-done.2 = bf16[4,1024,128]{2,1,0:T(8,128)(2,1)S(1)} async-done(((bf16[4,1024,128]{2,1,0:T(8,128)(2,1)}), bf16[4,1024,128]{2,1,0:T(8,128)(2,1)S(1)}, u32[]{:S(2)}, u32[]{:S(2)}) %all-to-all-start.2) | async-done | bytes 1048608 | tf_op jit(solution)/shard_map/all_to_all | solution.py:358
  145.3 1.0 copy-done.2
  146.3 17.3 %attend.1 = bf16[256,512]{1,0:T(8,128)(2,1)} custom-call(s32[2,8]{1,0:T(2,128)} %pad_add_fusion.bound_ref, bf16[8,256,128]{2,1,0:T(8,128)(2,1)} %prepare_queries.1.query_ref, bf16[4096,128]{1,0:T(8,128)(2,1)} %bitcast.45, s32[8,1,256]{2,1,0:T(1,128)} %tile.18.last_ref, bf16[256,256]{1,0:T(8,128)(2,1)} %get-tuple-element.11.unpick_ref), custom_call_target="tpu_custom_call" | custom-call | tf_op jit(solution)/shard_map/attend/pallas_call | solution.py:247
  163.6 13.6 %all_to_all.21 = bf16[8,32,512]{2,1,0:T(8,128)(2,1)S(1)} all-to-all(bf16[8,32,512]{2,1,0:T(8,128)(2,1)} %bitcast.48), channel_id=1, replica_groups=mesh['yh'=2,'z'=8,'x'=4,'yl'=4,'co'=2] {'yl','co'}, dimensions={0} | all-to-all | bytes 524288 | tf_op jit(solution)/shard_map/all_to_all | solution.py:361
  177.3 0.8 reshape.415
  (49 shorter events, 3.1 us)
Async XLA Ops:
  0.0 0.7 copy-start
  21.5 47.8 %copy-start.3 = (bf16[1,32,4096]{2,1,0:T(8,128)(2,1)S(1)}, bf16[1,32,4096]{2,1,0:T(8,128)(2,1)}, u32[]{:S(2)}) copy-start(bf16[1,32,4096]{2,1,0:T(8,128)(2,1)} %param.10) | copy-start | bytes 786436
  21.5 48.0 %copy-start.5 = (s32[1,32]{1,0:T(1,128)S(1)}, s32[1,32]{1,0:T(1,128)}, u32[]{:S(2)}) copy-start(s32[1,32]{1,0:T(1,128)} %param.12) | copy-start | bytes 388
  21.5 77.2 %collective-permute-start = (bf16[512,3072]{1,0:T(8,128)(2,1)}, bf16[512,3072]{1,0:T(8,128)(2,1)S(1)}, u32[]{:S(2)}, u32[]{:S(2)}) collective-permute-start(bf16[512,3072]{1,0:T(8,128)(2,1)} %reorder_hidden.1.own_ref), channel_id=1, source_target_pairs={{0,1},{1,0},{2,3},{3,2},{4,5},{5,4},{6,7},{7,6},{8,9},{9,8},{10,11... | collective-permute-start | bytes 9437192 | tf_op jit(solution)/shard_map/ppermute | solution.py:321
  31.7 62.0 %copy-start.4 = (f32[128]{0:T(128)S(1)}, f32[128]{0:T(128)}, u32[]{:S(2)}) copy-start(f32[128]{0:T(128)} %constant.89.clone) | copy-start | bytes 1540
  62.8 20.9 %collective-permute-start.1 = (bf16[768,512]{1,0:T(8,128)(2,1)}, bf16[768,512]{1,0:T(8,128)(2,1)}, u32[]{:S(2)}, u32[]{:S(2)}) collective-permute-start(bf16[768,512]{1,0:T(8,128)(2,1)} %bitcast.12.rest_0_), channel_id=1, source_target_pairs={{0,8},{8,16},{16,24},{24,0},{1,9},{9,17},{17,25},{25,1},{2,10},{10... | collective-permute-start | bytes 2359304 | tf_op jit(solution)/shard_map/ppermute | solution.py:277
  65.9 21.5 %collective-permute-start.2 = (bf16[768,512]{1,0:T(8,128)(2,1)}, bf16[768,512]{1,0:T(8,128)(2,1)}, u32[]{:S(2)}, u32[]{:S(2)}) collective-permute-start(bf16[768,512]{1,0:T(8,128)(2,1)} %bitcast.12.rest_0_), channel_id=1, source_target_pairs={{0,24},{8,0},{16,8},{24,16},{1,25},{9,1},{17,9},{25,17},{2,26},{10... | collective-permute-start | bytes 2359304 | tf_op jit(solution)/shard_map/ppermute | solution.py:278
  70.5 42.4 %all-to-all-start = ((bf16[8,32,640]{2,1,0:T(8,128)(2,1)}), bf16[8,32,640]{2,1,0:T(8,128)(2,1)S(1)}, u32[]{:S(2)}, u32[]{:S(2)}) async-start(bf16[8,32,640]{2,1,0:T(8,128)(2,1)} %maximum_bitcast_fusion), calls=%async_computation | async-start | bytes 655360 | tf_op jit(solution)/shard_map/all_to_all | solution.py:317
  85.4 22.0 %collective-permute-start.3 = (bf16[384,512]{1,0:T(8,128)(2,1)}, bf16[384,512]{1,0:T(8,128)(2,1)}, u32[]{:S(2)}, u32[]{:S(2)}) collective-permute-start(bf16[384,512]{1,0:T(8,128)(2,1)} %slice.37), channel_id=1, source_target_pairs={{0,8},{8,16},{16,24},{24,0},{1,9},{9,17},{17,25},{25,1},{2,10},{10... | collective-permute-start | bytes 1179656 | tf_op jit(solution)/shard_map/ppermute | solution.py:279
  89.2 18.3 %collective-permute-start.4 = (bf16[384,512]{1,0:T(8,128)(2,1)}, bf16[384,512]{1,0:T(8,128)(2,1)}, u32[]{:S(2)}, u32[]{:S(2)}) collective-permute-start(bf16[384,512]{1,0:T(8,128)(2,1)} %slice.38), channel_id=1, source_target_pairs={{0,24},{8,0},{16,8},{24,16},{1,25},{9,1},{17,9},{25,17},{2,26},{10... | collective-permute-start | bytes 1179656 | tf_op jit(solution)/shard_map/ppermute | solution.py:280
  98.7 1.7 copy-start.1
  112.8 32.5 %all-to-all-start.2 = ((bf16[4,1024,128]{2,1,0:T(8,128)(2,1)}), bf16[4,1024,128]{2,1,0:T(8,128)(2,1)S(1)}, u32[]{:S(2)}, u32[]{:S(2)}) async-start(bf16[4,1024,128]{2,1,0:T(8,128)(2,1)} %project.1), calls=%async_computation.2 | async-start | bytes 2097152 | tf_op jit(solution)/shard_map/all_to_all | solution.py:358
  145.3 1.0 copy-start.2

commit v3 on v2

--- a/solution.py
+++ b/solution.py
@@ -56,6 +56,7 @@
         out_specs=pl.BlockSpec((rows, tile), lambda i: (0, i)),
         out_shape=jax.ShapeDtypeStruct((rows, columns), jnp.bfloat16),
         name="reorder_hidden",
+        compiler_params=pltpu.CompilerParams(vmem_limit_bytes=16 << 20),
     )(source, hidden)
 
 
@@ -103,6 +104,7 @@
         out_specs=vmem,
         out_shape=jax.ShapeDtypeStruct((2 * own.shape[0], pieces[0].shape[1]), jnp.float32),
         name="first_half",
+        compiler_params=pltpu.CompilerParams(vmem_limit_bytes=20 << 20),
     )(core, own, other, *pieces)
 
 
@@ -137,6 +139,7 @@
         out_specs=vmem,
         out_shape=jax.ShapeDtypeStruct((heads, 2 * rows, LANES), jnp.bfloat16),
         name="project",
+        compiler_params=pltpu.CompilerParams(vmem_limit_bytes=20 << 20),
     )(core, own, other, total, cosine, sine, *pieces)
 
 
@@ -171,59 +174,60 @@
             (rows // QUERY_BLOCK, GROUP * QUERY_BLOCK, LANES), jnp.bfloat16
         ),
         name="prepare_queries",
+        compiler_params=pltpu.CompilerParams(vmem_limit_bytes=6 << 20),
     )(query, pick, cosine, sine)
 
 
 def attend_kernel(
-    bound_ref, query_ref, kv_ref, last_ref, unpick_ref, out_ref, value_ref, score_ref, sorted_ref
+    bound_ref, query_ref, kv_ref, last_ref, unpick_ref, out_ref, value_ref, even_ref, odd_ref, sorted_ref
 ):
     blocks = query_ref.shape[0]
     rows = query_ref.shape[1]
     keys = kv_ref.shape[0]
-    lane_kv = lax.broadcasted_iota(jnp.int32, (KEY_BLOCK, LANES), 1)
+    value_ref[WIDTH:, :] = jnp.ones((value_ref.shape[0] - WIDTH, keys), jnp.bfloat16)
     for step in range(keys // KEY_BLOCK):
         here = slice(step * KEY_BLOCK, (step + 1) * KEY_BLOCK)
-        value_ref[:, here] = jnp.where(
-            lane_kv < WIDTH, 1.0, kv_ref[here, :].astype(jnp.float32)
-        ).T.astype(jnp.bfloat16)
+        value_ref[:WIDTH, here] = kv_ref[here, :].T[WIDTH:]
     key_index = lax.broadcasted_iota(jnp.int32, (KEY_BLOCK, rows), 0)
     lane = lax.broadcasted_iota(jnp.int32, (QUERY_BLOCK, LANES), 1)
-
-    def one_block(block, carry):
-        query = query_ref[block]
-        last = last_ref[block]
+    no_top = jnp.full((8, rows), -1e30, jnp.float32)
+    no_total = jnp.zeros((value_ref.shape[0], rows), jnp.float32)
+
+    def score(score_ref, block, masked, index, top):
+        base = pl.multiple_of(index * KEY_BLOCK, KEY_BLOCK)
+        scores = lax.dot_general(
+            kv_ref[pl.ds(base, KEY_BLOCK), :],
+            query_ref[block],
+            (((1,), (1,)), ((), ())),
+            preferred_element_type=jnp.float32,
+        )
+        scores = scores * LOG2_E
+        if masked:
+            scores = jnp.where(key_index <= last_ref[block] - base, scores, -1e30)
+        score_ref[pl.ds(base, KEY_BLOCK), :] = scores
+        return jnp.maximum(top, jnp.max(scores.reshape(-1, 8, rows), axis=0))
+
+    def weigh(score_ref, top, index, total):
+        base = pl.multiple_of(index * KEY_BLOCK, KEY_BLOCK)
+        expo = jnp.exp2(score_ref[pl.ds(base, KEY_BLOCK), :] - top)
+        return total + jnp.dot(
+            value_ref[:, pl.ds(base, KEY_BLOCK)],
+            expo.astype(jnp.bfloat16),
+            preferred_element_type=jnp.float32,
+        )
+
+    def score_range(score_ref, block, begin, top):
         full, count = bound_ref[0, block], bound_ref[1, block]
-
-        def score(masked, index, top):
-            base = pl.multiple_of(index * KEY_BLOCK, KEY_BLOCK)
-            scores = lax.dot_general(
-                kv_ref[pl.ds(base, KEY_BLOCK), :],
-                query,
-                (((1,), (1,)), ((), ())),
-                preferred_element_type=jnp.float32,
-            )
-            scores = scores * LOG2_E
-            if masked:
-                scores = jnp.where(key_index <= last - base, scores, -1e30)
-            score_ref[pl.ds(base, KEY_BLOCK), :] = scores
-            return jnp.maximum(top, jnp.max(scores.reshape(-1, 8, rows), axis=0))
-
-        top = jnp.full((8, rows), -1e30, jnp.float32)
-        top = lax.fori_loop(0, full, functools.partial(score, False), top)
-        top = lax.fori_loop(full, count, functools.partial(score, True), top)
-        top = jnp.max(top, axis=0, keepdims=True)
-
-        def weigh(index, total):
-            base = pl.multiple_of(index * KEY_BLOCK, KEY_BLOCK)
-            expo = jnp.exp2(score_ref[pl.ds(base, KEY_BLOCK), :] - top)
-            return total + jnp.dot(
-                value_ref[:, pl.ds(base, KEY_BLOCK)],
-                expo.astype(jnp.bfloat16),
-                preferred_element_type=jnp.float32,
-            )
-
-        total = lax.fori_loop(0, count, weigh, jnp.zeros((LANES, rows), jnp.float32))
-        result = total[WIDTH:] / total[:WIDTH]
+        middle = jnp.maximum(begin, full)
+        top = lax.fori_loop(
+            begin, middle, functools.partial(score, score_ref, block, False), top
+        )
+        return lax.fori_loop(
+            middle, count, functools.partial(score, score_ref, block, True), top
+        )
+
+    def finish(block, total):
+        result = total[:WIDTH] / total[WIDTH : WIDTH + 1]
         result = jnp.concatenate([result, result], 0).T
         place = pl.multiple_of(block * QUERY_BLOCK, QUERY_BLOCK)
         for pair in range(GROUP // 2):
@@ -232,9 +236,37 @@
             sorted_ref[pl.ds(place, QUERY_BLOCK), pair * LANES : (pair + 1) * LANES] = jnp.where(
                 lane < WIDTH, even, odd
             ).astype(jnp.bfloat16)
-        return carry
-
-    lax.fori_loop(0, blocks, one_block, 0)
+
+    def one_block(here_ref, next_ref, block, top):
+        top = jnp.max(top, axis=0, keepdims=True)
+        count = bound_ref[1, block]
+        middle = jnp.minimum(count, bound_ref[0, block + 1])
+
+        def both(masked, index, state):
+            next_top, total = state
+            return (
+                score(next_ref, block + 1, masked, index, next_top),
+                weigh(here_ref, top, index, total),
+            )
+
+        state = lax.fori_loop(0, middle, functools.partial(both, False), (no_top, no_total))
+        state = lax.fori_loop(middle, count, functools.partial(both, True), state)
+        finish(block, state[1])
+        return score_range(next_ref, block + 1, count, state[0])
+
+    def two_blocks(pair, top):
+        top = one_block(even_ref, odd_ref, 2 * pair, top)
+        return one_block(odd_ref, even_ref, 2 * pair + 1, top)
+
+    top = score_range(even_ref, 0, 0, no_top)
+    top = lax.fori_loop(0, blocks // 2 - 1, two_blocks, top)
+    top = one_block(even_ref, odd_ref, blocks - 2, top)
+    top = jnp.max(top, axis=0, keepdims=True)
+    final = blocks - 1
+    total = lax.fori_loop(
+        0, bound_ref[1, final], functools.partial(weigh, odd_ref, top), no_total
+    )
+    finish(final, total)
     out_ref[...] = jnp.dot(
         unpick_ref[...], sorted_ref[...], preferred_element_type=jnp.float32
     ).astype(jnp.bfloat16)
@@ -250,11 +282,13 @@
         out_specs=vmem,
         out_shape=jax.ShapeDtypeStruct((count, GROUP * WIDTH), jnp.bfloat16),
         scratch_shapes=[
-            pltpu.VMEM((LANES, keys), jnp.bfloat16),
+            pltpu.VMEM((WIDTH + 16, keys), jnp.bfloat16),
+            pltpu.VMEM((keys, query.shape[1]), jnp.float32),
             pltpu.VMEM((keys, query.shape[1]), jnp.float32),
             pltpu.VMEM((count, GROUP * WIDTH), jnp.bfloat16),
         ],
         name="attend",
+        compiler_params=pltpu.CompilerParams(vmem_limit_bytes=18 << 20),
     )(bounds, query, kv, last, unpick)
 
 
@@ -316,6 +350,14 @@
     payload = jnp.concatenate([queries[0].reshape(query_rows, KV_HEADS, GROUP * WIDTH), extra], -1)
     payload = lax.all_to_all(payload.transpose(1, 0, 2), SEQ, 0, 0, tiled=True)
 
+    sign = jnp.asarray(np.where(np.arange(LANES) % WIDTH < WIDTH // 2, -1.0, 1.0), jnp.float32)
+    freq = lane_frequencies(LANES)
+    is_key = jnp.arange(LANES) < WIDTH
+    chip_rows = 2 * rows
+    chip_pos = start + chip_rows * lax.axis_index("yl") + jnp.arange(chip_rows)
+    key_angle = chip_pos.astype(jnp.float32)[:, None] * jnp.where(is_key, freq, 0.0)[None, :]
+    key_cosine = jnp.cos(key_angle)
+    key_sine = jnp.sin(key_angle) * jnp.where(is_key, sign, 0.0)
     near, far = gather_weight(blocks)
     own = reorder(hidden[0], source)
     other = lax.ppermute(own, "co", ring(2, 1))
@@ -341,20 +383,12 @@
     bounds = jnp.stack([(by_block[:, 0] + 1) // KEY_BLOCK, by_block[:, -1] // KEY_BLOCK + 1])
     last_rows = jnp.tile(by_block, (1, GROUP))[:, None, :]
 
-    sign = jnp.asarray(np.where(np.arange(LANES) % WIDTH < WIDTH // 2, -1.0, 1.0), jnp.float32)
-    freq = lane_frequencies(LANES)
     query_angle = sorted_pos.astype(jnp.float32)[:, None] * freq[None, :]
     prepared = prepare(query, pick, jnp.cos(query_angle), jnp.sin(query_angle) * sign)
 
-    is_key = jnp.arange(LANES) < WIDTH
-    chip_rows = 2 * rows
-    chip_pos = start + chip_rows * lax.axis_index("yl") + jnp.arange(chip_rows)
-    key_angle = chip_pos.astype(jnp.float32)[:, None] * jnp.where(is_key, freq, 0.0)[None, :]
-    key_sine = jnp.sin(key_angle) * jnp.where(is_key, sign, 0.0)
-
     place = core.reshape(1)
     total = first_half(place, own, other, near)
-    kv = project(place, own, other, far, total, jnp.cos(key_angle), key_sine)
+    kv = project(place, own, other, far, total, key_cosine, key_sine)
     kv = lax.all_to_all(kv, "yl", 0, 0, tiled=True).reshape(keys, LANES)
     context = attend(bounds, prepared, kv, last_rows, unpick)
     context = context.reshape(seq, query_rows, GROUP * WIDTH)

time: 179 us -> 165 us (0.922)
  Pallas kernels: 46.9 us -> 32.3 us
  waiting for transfers between devices: 21.4 us -> 24.7 us
    pallas_call x1, Pallas kernels: 17.3 us -> 11.6 us  [attend(): pl.pallas_call(attend_kernel, in_specs=[pl.BlockSpec(memory_space=pltpu.S...]
    all_to_all x1, waiting for transfers between devices: 18 us -> 21.2 us  [attention(): kv = lax.all_to_all(kv, 'yl', 0, 0, tiled=True).reshape(keys, LANES)]
    pallas_call x1, Pallas kernels: 14.6 us -> 12.2 us  [reorder(): pl.pallas_call(reorder_kernel, grid=(columns // tile,), in_specs=[pl.Bloc...]
    pallas_call x1, Pallas kernels: 5.33 us -> 3.05 us  [project(): pl.pallas_call(project_kernel, grid=(1,), in_specs=[pl.BlockSpec(memory_s...]
    pallas_call x1, Pallas kernels: 7.12 us -> 4.95 us  [first_half(): pl.pallas_call(first_half_kernel, grid=(1,), in_specs=[pl.BlockSpec(memor...]
    pallas_call x1, Pallas kernels: 2.52 us -> 0.61 us  [prepare(): pl.pallas_call(prepare_kernel, in_specs=[vmem] * 4, out_specs=vmem, out_s...]
  transfers between devices with their start and end apart: 7 -> 7, of which waited for: 2 -> 2; matrix products, arithmetic and copies ran while one was open for 9% -> 8% of each run, Pallas kernels for 8% -> 5%
where the time goes in v3:
time: 165 us; the launch traced here: 164 us
  blocking collectives  44.3 us (27%)
  starting transfers between devices  38.8 us (24%)
  Pallas kernels  32.3 us (20%)
  waiting for transfers between devices  24.7 us (15%)
  local copies, waits for them, and re-layouts  17.3 us (10%)
  other arithmetic  5.93 us (4%)
    all_to_all x1, blocking collectives, spread(): whole = lax.all_to_all(copies, axis, 0, 0, tiled=True)  31 us
    all_to_all x1, waiting for transfers between devices, attention(): kv = lax.all_to_all(kv, 'yl', 0, 0, tiled=True).reshape(keys, LANES)  21.2 us
    all_to_all x1, blocking collectives, attention(): context = lax.all_to_all(context, SEQ, 0, 0, tiled=True)  13.3 us
    pallas_call x1, Pallas kernels, reorder(): pl.pallas_call(reorder_kernel, grid=(columns // tile,), in_specs=[pl.Bloc...  12.2 us
    pallas_call x1, Pallas kernels, attend(): pl.pallas_call(attend_kernel, in_specs=[pl.BlockSpec(memory_space=pltpu.S...  11.6 us
    all_to_all x1, starting transfers between devices, attention(): payload = lax.all_to_all(payload.transpose(1, 0, 2), SEQ, 0, 0, tiled=True)  9.63 us
    ppermute x1, starting transfers between devices, attention(): other = lax.ppermute(own, 'co', ring(2, 1))  8.88 us
    unnamed x16, local copies, waits for them, and re-layouts  7.92 us
  transfers between devices with their start and end apart: 7, of which 2 were waited for; matrix products, arithmetic and copies ran while one was open for 8% of the time, Pallas kernels for 5%

profile of v3, /device:TPU:1, one launch (start us, length us, event | category | flops | bytes accessed | tf_op | source)
XLA Modules:
  0.0 164.3 jit_solution(3720559364389120216)
XLA Ops:
  0.3 0.4 copy-done
  0.7 0.8 gather_fusion
  1.6 4.6 %copy.21 = bf16[1,512,2880]{2,1,0:T(8,128)(2,1)} copy(bf16[1,512,2880]{1,2,0:T(8,128)(2,1)} %param.7) | data formatting | bytes 5898240 | tf_op args[0]
  6.2 1.9 %copy-done.1 = bf16[1,512,2880]{2,1,0:T(8,128)(2,1)S(1)} copy-done((bf16[1,512,2880]{2,1,0:T(8,128)(2,1)S(1)}, bf16[1,512,2880]{2,1,0:T(8,128)(2,1)}, u32[]{:S(2)}) %copy-start.1) | copy-done | bytes 2949144
  8.1 12.2 %reorder_hidden.1.own_ref = bf16[512,3072]{1,0:T(8,128)(2,1)S(1)} custom-call(s32[1,3072]{1,0:T(1,128)S(1)} %select_n.83.source_ref, bf16[512,2880]{1,0:T(8,128)(2,1)S(1)} %bitcast.44), custom_call_target="tpu_custom_call" | custom-call | tf_op jit(solution)/shard_map/reorder_hidden/pallas_call | solution.py:49
  20.3 8.9 %collective-permute-start = (bf16[512,3072]{1,0:T(8,128)(2,1)S(1)}, bf16[512,3072]{1,0:T(8,128)(2,1)}, u32[]{:S(2)}, u32[]{:S(2)}) collective-permute-start(bf16[512,3072]{1,0:T(8,128)(2,1)S(1)} %reorder_hidden.1.own_ref), channel_id=1, source_target_pairs={{0,1},{1,0},{2,3},{3,2},{4,5},{5,4},{6,7},{7,6},{8,9},{9,8},{10,11... | collective-permute-start | bytes 9437192 | tf_op jit(solution)/shard_map/ppermute | solution.py:363
  29.2 0.9 reshape.410
  30.5 31.0 %all_to_all.20 = bf16[16,48,512]{2,1,0:T(8,128)(2,1)} all-to-all(bf16[16,48,512]{2,1,0:T(8,128)(2,1)S(1)} %broadcast_in_dim.35), channel_id=1, replica_groups=mesh['yh'=2,'z'=8,'x'=4,'yl'=4,'co'=2] {'yh','z'}, dimensions={0} | all-to-all | bytes 1572864 | tf_op jit(solution)/shard_map/all_to_all | solution.py:298
  61.5 3.1 %collective-permute-start.1 = (bf16[768,512]{1,0:T(8,128)(2,1)}, bf16[768,512]{1,0:T(8,128)(2,1)}, u32[]{:S(2)}, u32[]{:S(2)}) collective-permute-start(bf16[768,512]{1,0:T(8,128)(2,1)} %bitcast.12.rest_0_), channel_id=1, source_target_pairs={{0,8},{8,16},{16,24},{24,0},{1,9},{9,17},{17,25},{25,1},{2,10},{10... | collective-permute-start | bytes 2359304 | tf_op jit(solution)/shard_map/ppermute | solution.py:311
  64.6 3.4 %collective-permute-start.2 = (bf16[768,512]{1,0:T(8,128)(2,1)}, bf16[768,512]{1,0:T(8,128)(2,1)}, u32[]{:S(2)}, u32[]{:S(2)}) collective-permute-start(bf16[768,512]{1,0:T(8,128)(2,1)} %bitcast.12.rest_0_), channel_id=1, source_target_pairs={{0,24},{8,0},{16,8},{24,16},{1,25},{9,1},{17,9},{25,17},{2,26},{10... | collective-permute-start | bytes 2359304 | tf_op jit(solution)/shard_map/ppermute | solution.py:312
  68.4 0.8 maximum_bitcast_fusion
  69.2 9.6 %all-to-all-start = ((bf16[8,32,640]{2,1,0:T(8,128)(2,1)}), bf16[8,32,640]{2,1,0:T(8,128)(2,1)}, u32[]{:S(2)}, u32[]{:S(2)}) async-start(bf16[8,32,640]{2,1,0:T(8,128)(2,1)} %maximum_bitcast_fusion), calls=%async_computation | async-start | bytes 655360 | tf_op jit(solution)/shard_map/all_to_all | solution.py:351
  79.0 3.4 %collective-permute-done.1.rest_1_ = bf16[768,512]{1,0:T(8,128)(2,1)} collective-permute-done((bf16[768,512]{1,0:T(8,128)(2,1)}, bf16[768,512]{1,0:T(8,128)(2,1)}, u32[]{:S(2)}, u32[]{:S(2)}) %collective-permute-start.1) | collective-permute-done | bytes 786464 | tf_op jit(solution)/shard_map/ppermute | solution.py:311
  82.4 1.8 %slice.37 = bf16[384,512]{1,0:T(8,128)(2,1)} slice(bf16[768,512]{1,0:T(8,128)(2,1)} %collective-permute-done.1.rest_1_), slice={[0:384], [0:512]} | slice | bytes 786432 | tf_op jit(solution)/shard_map/slice | solution.py:313
  84.2 1.9 %collective-permute-start.3 = (bf16[384,512]{1,0:T(8,128)(2,1)}, bf16[384,512]{1,0:T(8,128)(2,1)S(1)}, u32[]{:S(2)}, u32[]{:S(2)}) collective-permute-start(bf16[384,512]{1,0:T(8,128)(2,1)} %slice.37), channel_id=1, source_target_pairs={{0,8},{8,16},{16,24},{24,0},{1,9},{9,17},{17,25},{25,1},{2,10},{10... | collective-permute-start | bytes 1179656 | tf_op jit(solution)/shard_map/ppermute | solution.py:313
  86.1 1.8 %slice.38 = bf16[384,512]{1,0:T(8,128)(2,1)} slice(bf16[768,512]{1,0:T(8,128)(2,1)} %collective-permute-done.2.rest_2_), slice={[384:768], [0:512]} | slice | bytes 786432 | tf_op jit(solution)/shard_map/slice | solution.py:314
  87.9 4.6 %collective-permute-start.4 = (bf16[384,512]{1,0:T(8,128)(2,1)}, bf16[384,512]{1,0:T(8,128)(2,1)}, u32[]{:S(2)}, u32[]{:S(2)}) collective-permute-start(bf16[384,512]{1,0:T(8,128)(2,1)} %slice.38), channel_id=1, source_target_pairs={{0,24},{8,0},{16,8},{24,16},{1,25},{9,1},{17,9},{25,17},{2,26},{10... | collective-permute-start | bytes 1179656 | tf_op jit(solution)/shard_map/ppermute | solution.py:314
  92.4 0.7 compare_select_fusion.9
  93.1 1.2 slice.26
  94.9 1.9 %fusion = (f32[1024,128]{1,0:T(8,128)S(1)}, f32[1024,128]{1,0:T(8,128)S(1)}) fusion(f32[128]{0:T(128)S(1)} %get-tuple-element.19, f32[128]{0:T(128)S(1)} %get-tuple-element.20, f32[1024]{0:T(1024)S(1)} %add_convert_fusion), kind=kLoop, calls=%fused_computation.3 | loop fusion | flops 262144 | bytes 1053696 | tf_op jit(solution)/shard_map/mul | solution.py:360
  96.9 4.9 %first_half.1.total_ref = f32[1024,512]{1,0:T(8,128)S(1)} custom-call(s32[1]{0:T(128)} %bitcast.5.core_ref, bf16[512,3072]{1,0:T(8,128)(2,1)S(1)} %reorder_hidden.1.own_ref, bf16[512,3072]{1,0:T(8,128)(2,1)} %collective-permute-done.other_ref, bf16[768,512]{1,0:T(8,128)(2,1)} %bitcast.12.rest_0_, bf16[768,512]{1,0:T(8,128)(2,1)} %collective-permute-done.1.rest_1_, ...), custom_call_target="tpu_custom_call" | custom-call | tf_op jit(solution)/shard_map/first_half/pallas_call | solution.py:100
  101.8 3.0 %project.1 = bf16[4,1024,128]{2,1,0:T(8,128)(2,1)S(1)} custom-call(s32[1]{0:T(128)} %bitcast.5.core_ref, bf16[512,3072]{1,0:T(8,128)(2,1)S(1)} %reorder_hidden.1.own_ref, bf16[512,3072]{1,0:T(8,128)(2,1)} %collective-permute-done.other_ref, f32[1024,512]{1,0:T(8,128)S(1)} %first_half.1.total_ref, f32[1024,128]{1,0:T(8,128)S(1)} %get-tuple-element.8.cos_ref, ...), custom_call_target="tpu_custom_call" | custom-call | tf_op jit(solution)/shard_map/project/pallas_call | solution.py:134
  104.9 1.0 copy-done.2
  105.9 7.3 %all-to-all-start.2 = ((bf16[4,1024,128]{2,1,0:T(8,128)(2,1)}), bf16[4,1024,128]{2,1,0:T(8,128)(2,1)S(1)}, u32[]{:S(2)}, u32[]{:S(2)}) async-start(bf16[4,1024,128]{2,1,0:T(8,128)(2,1)} %copy-done.2), calls=%async_computation.2 | async-start | bytes 2097152 | tf_op jit(solution)/shard_map/all_to_all | solution.py:392
  113.2 1.0 slice.36.query_ref
  114.1 1.1 convert_reduce_fusion.1
  115.9 0.5 fusion.5
  116.4 0.6 prepare_queries.1.query_ref
  117.2 21.2 %all-to-all-done.2 = bf16[4,1024,128]{2,1,0:T(8,128)(2,1)S(1)} async-done(((bf16[4,1024,128]{2,1,0:T(8,128)(2,1)}), bf16[4,1024,128]{2,1,0:T(8,128)(2,1)S(1)}, u32[]{:S(2)}, u32[]{:S(2)}) %all-to-all-start.2) | async-done | bytes 1048608 | tf_op jit(solution)/shard_map/all_to_all | solution.py:392
  138.5 11.6 %attend.1 = bf16[256,512]{1,0:T(8,128)(2,1)S(1)} custom-call(s32[2,8]{1,0:T(2,128)S(1)} %pad_add_fusion.bound_ref, bf16[8,256,128]{2,1,0:T(8,128)(2,1)S(1)} %prepare_queries.1.query_ref, bf16[4096,128]{1,0:T(8,128)(2,1)S(1)} %bitcast.45, s32[8,1,256]{2,1,0:T(1,128)S(1)} %tile.18.last_ref, bf16[256,256]{1,0:T(8,128)(2,1)S(1)} %get-tuple-element.11.unpick_ref), custom_call_target="tpu_custom_call" | custom-call | tf_op jit(solution)/shard_map/attend/pallas_call | solution.py:279
  150.0 13.3 %all_to_all.21 = bf16[8,32,512]{2,1,0:T(8,128)(2,1)S(1)} all-to-all(bf16[8,32,512]{2,1,0:T(8,128)(2,1)S(1)} %bitcast.46), channel_id=1, replica_groups=mesh['yh'=2,'z'=8,'x'=4,'yl'=4,'co'=2] {'yl','co'}, dimensions={0} | all-to-all | bytes 524288 | tf_op jit(solution)/shard_map/all_to_all | solution.py:395
  163.5 0.8 reshape.415
  (49 shorter events, 2.3 us)
Async XLA Ops:
  0.0 0.7 copy-start
  6.2 1.9 %copy-start.1 = (bf16[1,512,2880]{2,1,0:T(8,128)(2,1)S(1)}, bf16[1,512,2880]{2,1,0:T(8,128)(2,1)}, u32[]{:S(2)}) copy-start(bf16[1,512,2880]{2,1,0:T(8,128)(2,1)} %copy.21) | copy-start | bytes 8847364
  20.2 47.8 %copy-start.3 = (bf16[1,32,4096]{2,1,0:T(8,128)(2,1)S(1)}, bf16[1,32,4096]{2,1,0:T(8,128)(2,1)}, u32[]{:S(2)}) copy-start(bf16[1,32,4096]{2,1,0:T(8,128)(2,1)} %param.10) | copy-start | bytes 786436
  20.3 48.0 %copy-start.5 = (s32[1,32]{1,0:T(1,128)S(1)}, s32[1,32]{1,0:T(1,128)}, u32[]{:S(2)}) copy-start(s32[1,32]{1,0:T(1,128)} %param.12) | copy-start | bytes 388
  20.3 76.6 %collective-permute-start = (bf16[512,3072]{1,0:T(8,128)(2,1)S(1)}, bf16[512,3072]{1,0:T(8,128)(2,1)}, u32[]{:S(2)}, u32[]{:S(2)}) collective-permute-start(bf16[512,3072]{1,0:T(8,128)(2,1)S(1)} %reorder_hidden.1.own_ref), channel_id=1, source_target_pairs={{0,1},{1,0},{2,3},{3,2},{4,5},{5,4},{6,7},{7,6},{8,9},{9,8},{10,11... | collective-permute-start | bytes 9437192 | tf_op jit(solution)/shard_map/ppermute | solution.py:363
  61.5 20.9 %collective-permute-start.1 = (bf16[768,512]{1,0:T(8,128)(2,1)}, bf16[768,512]{1,0:T(8,128)(2,1)}, u32[]{:S(2)}, u32[]{:S(2)}) collective-permute-start(bf16[768,512]{1,0:T(8,128)(2,1)} %bitcast.12.rest_0_), channel_id=1, source_target_pairs={{0,8},{8,16},{16,24},{24,0},{1,9},{9,17},{17,25},{25,1},{2,10},{10... | collective-permute-start | bytes 2359304 | tf_op jit(solution)/shard_map/ppermute | solution.py:311
  64.6 21.5 %collective-permute-start.2 = (bf16[768,512]{1,0:T(8,128)(2,1)}, bf16[768,512]{1,0:T(8,128)(2,1)}, u32[]{:S(2)}, u32[]{:S(2)}) collective-permute-start(bf16[768,512]{1,0:T(8,128)(2,1)} %bitcast.12.rest_0_), channel_id=1, source_target_pairs={{0,24},{8,0},{16,8},{24,16},{1,25},{9,1},{17,9},{25,17},{2,26},{10... | collective-permute-start | bytes 2359304 | tf_op jit(solution)/shard_map/ppermute | solution.py:312
  69.2 36.6 %all-to-all-start = ((bf16[8,32,640]{2,1,0:T(8,128)(2,1)}), bf16[8,32,640]{2,1,0:T(8,128)(2,1)}, u32[]{:S(2)}, u32[]{:S(2)}) async-start(bf16[8,32,640]{2,1,0:T(8,128)(2,1)} %maximum_bitcast_fusion), calls=%async_computation | async-start | bytes 655360 | tf_op jit(solution)/shard_map/all_to_all | solution.py:351
  84.2 17.6 %collective-permute-start.3 = (bf16[384,512]{1,0:T(8,128)(2,1)}, bf16[384,512]{1,0:T(8,128)(2,1)S(1)}, u32[]{:S(2)}, u32[]{:S(2)}) collective-permute-start(bf16[384,512]{1,0:T(8,128)(2,1)} %slice.37), channel_id=1, source_target_pairs={{0,8},{8,16},{16,24},{24,0},{1,9},{9,17},{17,25},{25,1},{2,10},{10... | collective-permute-start | bytes 1179656 | tf_op jit(solution)/shard_map/ppermute | solution.py:313
  87.9 13.9 %collective-permute-start.4 = (bf16[384,512]{1,0:T(8,128)(2,1)}, bf16[384,512]{1,0:T(8,128)(2,1)}, u32[]{:S(2)}, u32[]{:S(2)}) collective-permute-start(bf16[384,512]{1,0:T(8,128)(2,1)} %slice.38), channel_id=1, source_target_pairs={{0,24},{8,0},{16,8},{24,16},{1,25},{9,1},{17,9},{25,17},{2,26},{10... | collective-permute-start | bytes 1179656 | tf_op jit(solution)/shard_map/ppermute | solution.py:314
  104.9 1.0 copy-start.2
  105.8 10.0 %copy-start.4 = (f32[128]{0:T(128)S(1)}, f32[128]{0:T(128)}, u32[]{:S(2)}) copy-start(f32[128]{0:T(128)} %constant.89.clone) | copy-start | bytes 1540
  105.9 32.6 %all-to-all-start.2 = ((bf16[4,1024,128]{2,1,0:T(8,128)(2,1)}), bf16[4,1024,128]{2,1,0:T(8,128)(2,1)S(1)}, u32[]{:S(2)}, u32[]{:S(2)}) async-start(bf16[4,1024,128]{2,1,0:T(8,128)(2,1)} %copy-done.2), calls=%async_computation.2 | async-start | bytes 2097152 | tf_op jit(solution)/shard_map/all_to_all | solution.py:392

commit v4 on v3

--- a/solution.py
+++ b/solution.py
@@ -33,23 +33,39 @@
     return [(i, (i + step) % size) for i in range(size)]
 
 
-def reorder_kernel(source_ref, hidden_ref, out_ref):
-    depth = hidden_ref.shape[1]
-    index = lax.broadcasted_iota(jnp.int32, (depth, source_ref.shape[1]), 0)
-    pick = jnp.where(index == source_ref[...], 1.0, 0.0).astype(jnp.bfloat16)
-    out_ref[...] = jnp.dot(
-        hidden_ref[...], pick, preferred_element_type=jnp.float32
-    ).astype(jnp.bfloat16)
-
-
-def reorder(hidden, source):
+def reorder_kernel(window_ref, source_ref, hidden_ref, out_ref):
+    group = pl.program_id(0)
+    index = lax.broadcasted_iota(jnp.int32, (2 * LANES, LANES), 0)
+    lane = lax.broadcasted_iota(jnp.int32, (1, LANES), 1)
+    slots = out_ref.shape[1] // PAD_ROWS
+    for tile in range(out_ref.shape[1] // LANES):
+        begin = tile * LANES
+        source = source_ref[:, begin : begin + LANES]
+        rows, picks = [], []
+        for slot in range(slots):
+            low, high = slot * PAD_ROWS - begin, (slot + 1) * PAD_ROWS - begin
+            if high <= 0 or low >= LANES:
+                continue
+            window = pl.multiple_of(window_ref[group * slots + slot], LANES)
+            place = jnp.where((lane >= low) & (lane < high), source - window, -1)
+            picks.append(jnp.where(index == place, 1.0, 0.0).astype(jnp.bfloat16))
+            rows.append(hidden_ref[:, pl.ds(window, 2 * LANES)])
+        out_ref[:, begin : begin + LANES] = jnp.dot(
+            jnp.concatenate(rows, 1),
+            jnp.concatenate(picks, 0),
+            preferred_element_type=jnp.float32,
+        ).astype(jnp.bfloat16)
+
+
+def reorder(hidden, source, window):
     rows, depth = hidden.shape
     columns = source.shape[1]
-    tile = 256
+    tile = 8 * PAD_ROWS
     return pl.pallas_call(
         reorder_kernel,
         grid=(columns // tile,),
         in_specs=[
+            pl.BlockSpec(memory_space=pltpu.SMEM),
             pl.BlockSpec((1, tile), lambda i: (0, i)),
             pl.BlockSpec((rows, depth), lambda i: (0, 0)),
         ],
@@ -57,7 +73,7 @@
         out_shape=jax.ShapeDtypeStruct((rows, columns), jnp.bfloat16),
         name="reorder_hidden",
         compiler_params=pltpu.CompilerParams(vmem_limit_bytes=16 << 20),
-    )(source, hidden)
+    )(window, source, hidden)
 
 
 def swap_halves(x, lane):
@@ -70,42 +86,44 @@
 
 
 def product(hidden_ref, pieces):
-    total, offset = None, 0
-    for piece in pieces:
-        size = piece.shape[0]
-        part = jnp.dot(
-            hidden_ref[:, offset : offset + size],
-            piece[...],
-            preferred_element_type=jnp.float32,
-        )
-        total = part if total is None else total + part
-        offset += size
-    return total
-
-
-def first_half_kernel(core_ref, own_ref, other_ref, *rest):
+    weight = jnp.concatenate([piece[...] for piece in pieces], 0)
+    return jnp.dot(hidden_ref[...], weight, preferred_element_type=jnp.float32)
+
+
+def partial_kernel(core_ref, own_ref, other_ref, *rest):
     pieces, out_ref = rest[:-1], rest[-1]
     rows = own_ref.shape[0]
     core = core_ref[0]
     for hidden_ref, place in ((own_ref, core), (other_ref, 1 - core)):
-        out_ref[pl.ds(pl.multiple_of(place * rows, rows), rows), :] = product(
-            hidden_ref, pieces
-        )
-
-
-def first_half(core, own, other, pieces):
+        here = pl.ds(pl.multiple_of(place * rows, rows), rows)
+        out_ref[here, :] = product(hidden_ref, pieces)
+
+
+def partial_sum_kernel(core_ref, own_ref, other_ref, total_ref, *rest):
+    pieces, out_ref = rest[:-1], rest[-1]
+    rows = own_ref.shape[0]
+    core = core_ref[0]
+    for hidden_ref, place in ((own_ref, core), (other_ref, 1 - core)):
+        here = pl.ds(pl.multiple_of(place * rows, rows), rows)
+        out_ref[here, :] = total_ref[here, :] + product(hidden_ref, pieces)
+
+
+def partial_product(core, own, other, pieces, *total):
     vmem = pl.BlockSpec(memory_space=pltpu.VMEM)
-    depth = sum(piece.shape[0] for piece in pieces)
-    part = pl.BlockSpec((own.shape[0], depth), lambda i: (0, 0))
-    return pl.pallas_call(
-        first_half_kernel,
+    rows = own.shape[0]
+    column = 0 if total else 2
+    part = pl.BlockSpec((rows, sum(p.shape[0] for p in pieces)), lambda i: (0, column))
+    return pl.pallas_call(
+        partial_sum_kernel if total else partial_kernel,
         grid=(1,),
-        in_specs=[pl.BlockSpec(memory_space=pltpu.SMEM), part, part] + [vmem] * len(pieces),
+        in_specs=[pl.BlockSpec(memory_space=pltpu.SMEM)]
+        + [part, part]
+        + [vmem] * (len(pieces) + len(total)),
         out_specs=vmem,
-        out_shape=jax.ShapeDtypeStruct((2 * own.shape[0], pieces[0].shape[1]), jnp.float32),
-        name="first_half",
-        compiler_params=pltpu.CompilerParams(vmem_limit_bytes=20 << 20),
-    )(core, own, other, *pieces)
+        out_shape=jax.ShapeDtypeStruct((2 * rows, pieces[0].shape[1]), jnp.float32),
+        name="middle_product" if total else "first_product",
+        compiler_params=pltpu.CompilerParams(vmem_limit_bytes=18 << 20),
+    )(core, own, other, *total, *pieces)
 
 
 def project_kernel(core_ref, own_ref, other_ref, total_ref, cos_ref, sin_ref, *rest):
@@ -292,11 +310,44 @@
     )(bounds, query, kv, last, unpick)
 
 
-def spread(x, axis):
-    size = lax.axis_size(axis)
-    copies = jnp.broadcast_to(x[None], (size,) + x.shape)
-    whole = lax.all_to_all(copies, axis, 0, 0, tiled=True)
+def mirrored_groups():
+    sizes = [lax.axis_size(axis) for axis in ("yh", "z", "yl")]
+    return [
+        [
+            (high * sizes[1] + z) * sizes[2] + (low if high == 0 else sizes[2] - 1 - low)
+            for high in range(sizes[0])
+            for z in range(sizes[1])
+        ]
+        for low in range(sizes[2])
+    ]
+
+
+def spread(x):
+    groups = mirrored_groups()
+    copies = jnp.broadcast_to(x[None], (len(groups[0]),) + x.shape)
+    whole = lax.all_to_all(
+        copies, ("yh", "z", "yl"), 0, 0, axis_index_groups=groups, tiled=True
+    )
     return whole.reshape((-1,) + x.shape[1:])
+
+
+def halves_kernel(whole_ref, low_ref, high_ref):
+    half = low_ref.shape[0]
+    low_ref[...] = whole_ref[:half]
+    high_ref[...] = whole_ref[half:]
+
+
+def halves(whole):
+    vmem = pl.BlockSpec(memory_space=pltpu.VMEM)
+    shape = jax.ShapeDtypeStruct((whole.shape[0] // 2, whole.shape[1]), whole.dtype)
+    return pl.pallas_call(
+        halves_kernel,
+        in_specs=[vmem],
+        out_specs=[vmem, vmem],
+        out_shape=[shape, shape],
+        name="halves",
+        compiler_params=pltpu.CompilerParams(vmem_limit_bytes=6 << 20),
+    )(whole)
 
 
 def gather_weight(blocks):
@@ -305,19 +356,29 @@
     split = blocks.reshape(block_rows, KV_HEADS // 2, 2, LANES)
     mine = lax.dynamic_index_in_dim(split, core, 2, False).reshape(block_rows, -1)
     mine = jnp.pad(mine, ((0, PAD_ROWS - block_rows), (0, 0)))
-    plane = spread(mine, ("yh", "z"))
-    half = plane.shape[0] // 2
+    plane = spread(mine)
     up, down = ring(4, 1), ring(4, -1)
-    below = lax.ppermute(plane, "x", up)
-    above = lax.ppermute(plane, "x", down)
-    low = lax.ppermute(below[:half], "x", up)
-    high = lax.ppermute(above[half:], "x", down)
-    return (plane, below, above), (low, high)
+    low, high = halves(plane)
+
+    def send(piece, pairs):
+        return lax.ppermute(piece, "x", pairs)
+
+    below_low = send(low, up)
+    above_high = send(high, down)
+    below_high = send(high, up)
+    above_low = send(low, down)
+    across_low = send(below_low, up)
+    across_high = send(above_high, down)
+    return (
+        (low, high),
+        (below_low, below_high, above_low, above_high),
+        (across_low, across_high),
+    )
 
 
 def slot_order(block_of):
     x = lax.axis_index("x")
-    xs = jnp.stack([x, x + 3, x + 1, x + 2]) % 4
+    xs = jnp.stack([x + 3, x + 1, x, x + 2]) % 4
     stored = jnp.arange(16)[None, :] * 4 + xs[:, None]
     return block_of[stored.reshape(-1)]
 
@@ -348,18 +409,26 @@
         -1,
     )
     payload = jnp.concatenate([queries[0].reshape(query_rows, KV_HEADS, GROUP * WIDTH), extra], -1)
-    payload = lax.all_to_all(payload.transpose(1, 0, 2), SEQ, 0, 0, tiled=True)
+    payload = payload.transpose(1, 0, 2)
+    payload = lax.all_to_all(payload, SEQ, 0, 0, tiled=True)
 
     sign = jnp.asarray(np.where(np.arange(LANES) % WIDTH < WIDTH // 2, -1.0, 1.0), jnp.float32)
     freq = lane_frequencies(LANES)
     is_key = jnp.arange(LANES) < WIDTH
-    chip_rows = 2 * rows
-    chip_pos = start + chip_rows * lax.axis_index("yl") + jnp.arange(chip_rows)
+    mine = key_pos[0]
+    theirs = mine + jnp.where(core == 0, rows, -rows)
+    chip_pos = jnp.where(
+        core == 0, jnp.concatenate([mine, theirs]), jnp.concatenate([theirs, mine])
+    )
     key_angle = chip_pos.astype(jnp.float32)[:, None] * jnp.where(is_key, freq, 0.0)[None, :]
     key_cosine = jnp.cos(key_angle)
     key_sine = jnp.sin(key_angle) * jnp.where(is_key, sign, 0.0)
-    near, far = gather_weight(blocks)
-    own = reorder(hidden[0], source)
+    plane, middle, far = gather_weight(blocks)
+    depth = hidden.shape[2]
+    wide = pl.cdiv(depth, LANES) * LANES
+    padded = jnp.pad(hidden[0], ((0, 0), (0, wide - depth)))
+    window = jnp.minimum(slots * block_rows // LANES * LANES, wide - 2 * LANES)
+    own = reorder(padded, source, window)
     other = lax.ppermute(own, "co", ring(2, 1))
 
     total_queries = query_rows * seq
@@ -387,7 +456,8 @@
     prepared = prepare(query, pick, jnp.cos(query_angle), jnp.sin(query_angle) * sign)
 
     place = core.reshape(1)
-    total = first_half(place, own, other, near)
+    total = partial_product(place, own, other, plane)
+    total = partial_product(place, own, other, middle, total)
     kv = project(place, own, other, far, total, key_cosine, key_sine)
     kv = lax.all_to_all(kv, "yl", 0, 0, tiled=True).reshape(keys, LANES)
     context = attend(bounds, prepared, kv, last_rows, unpick)

time: 165 us -> 156 us (0.945)
  blocking collectives: 44.3 us -> 12.6 us
  waiting for transfers between devices: 24.7 us -> 44.6 us
  starting transfers between devices: 38.8 us -> 46.3 us
  local copies, waits for them, and re-layouts: 17.3 us -> 11.8 us
  Pallas kernels: 32.3 us -> 30.6 us
    all_to_all x1 -> x0, blocking collectives: 31 us -> none  [spread(): whole = lax.all_to_all(copies, axis, 0, 0, tiled=True)]
    all_to_all x1 -> x2, waiting for transfers between devices: 0.01 us -> 22.5 us  [the longest x1 22.5 us: spread(): lax.all_to_all(copies, ('yh', 'z', 'yl'), 0, 0, axis_index_groups=groups,...]
    ppermute x4 -> x6, starting transfers between devices: 13 us -> 19.5 us  [send(): return lax.ppermute(piece, 'x', pairs)]
    pallas_call x1, Pallas kernels: 12.2 us -> 7.93 us  [reorder(): pl.pallas_call(reorder_kernel, grid=(columns // tile,), in_specs=[pl.Bloc...]
    all_to_all x1 -> x2, starting transfers between devices: 9.63 us -> 13.8 us  [the longest x1 7.76 us: spread(): lax.all_to_all(copies, ('yh', 'z', 'yl'), 0, 0, axis_index_groups=groups,...]
    slice x2 -> x0, local copies, waits for them, and re-layouts: 3.52 us -> none  [the longest x1 1.76 us: gather_weight(): high = lax.ppermute(above[half:], 'x', down)]
    all_to_all x1, starting transfers between devices: 7.31 us -> 4.16 us  [attention(): kv = lax.all_to_all(kv, 'yl', 0, 0, tiled=True).reshape(keys, LANES)]
    unnamed x16, local copies, waits for them, and re-layouts: 7.92 us -> 4.82 us
  transfers between devices with their start and end apart: 7 -> 10, of which waited for: 2 -> 4; matrix products, arithmetic and copies ran while one was open for 8% -> 8% of each run, Pallas kernels for 5% -> 7%
where the time goes in v4:
time: 156 us; the launch traced here: 154 us
  starting transfers between devices  46.3 us (30%)
  waiting for transfers between devices  44.6 us (29%)
  Pallas kernels  30.6 us (20%)
  blocking collectives  12.6 us (8%)
  local copies, waits for them, and re-layouts  11.8 us (8%)
  other arithmetic  6.89 us (4%)
    all_to_all x1, waiting for transfers between devices, spread(): lax.all_to_all(copies, ('yh', 'z', 'yl'), 0, 0, axis_index_groups=groups,...  22.5 us
    all_to_all x1, waiting for transfers between devices, attention(): kv = lax.all_to_all(kv, 'yl', 0, 0, tiled=True).reshape(keys, LANES)  20.1 us
    ppermute x6, starting transfers between devices, send(): return lax.ppermute(piece, 'x', pairs)  19.5 us
    all_to_all x1, blocking collectives, attention(): context = lax.all_to_all(context, SEQ, 0, 0, tiled=True)  12.6 us
    pallas_call x1, Pallas kernels, attend(): pl.pallas_call(attend_kernel, in_specs=[pl.BlockSpec(memory_space=pltpu.S...  11.5 us
    ppermute x1, starting transfers between devices, attention(): other = lax.ppermute(own, 'co', ring(2, 1))  8.88 us
    pallas_call x1, Pallas kernels, reorder(): pl.pallas_call(reorder_kernel, grid=(columns // tile,), in_specs=[pl.Bloc...  7.93 us
    all_to_all x1, starting transfers between devices, spread(): lax.all_to_all(copies, ('yh', 'z', 'yl'), 0, 0, axis_index_groups=groups,...  7.76 us
  transfers between devices with their start and end apart: 10, of which 4 were waited for; matrix products, arithmetic and copies ran while one was open for 8% of the time, Pallas kernels for 7%

profile of v4, /device:TPU:1, one launch (start us, length us, event | category | flops | bytes accessed | tf_op | source)
XLA Modules:
  0.0 153.9 jit_solution(1236765231476261958)
XLA Ops:
  0.7 0.8 gather_fusion
  1.6 3.3 %copy.21 = bf16[1,512,2880]{2,1,0:T(8,128)(2,1)S(1)} copy(bf16[1,512,2880]{1,2,0:T(8,128)(2,1)} %param.7) | data formatting | bytes 5898240 | tf_op args[0]
  5.2 7.9 %reorder_hidden.1.own_ref = bf16[512,3072]{1,0:T(8,128)(2,1)S(1)} custom-call(s32[64]{0:T(128)S(1)} %get-tuple-element.20.window_ref, s32[1,3072]{1,0:T(1,128)S(1)} %select_n.105.source_ref, bf16[512,2944]{1,0:T(8,128)(2,1)S(1)} %pad.8.hidden_ref), custom_call_target="tpu_custom_call" | custom-call | tf_op jit(solution)/shard_map/reorder_hidden/pallas_call | solution.py:64
  13.2 8.9 %collective-permute-start = (bf16[512,3072]{1,0:T(8,128)(2,1)S(1)}, bf16[512,3072]{1,0:T(8,128)(2,1)}, u32[]{:S(2)}, u32[]{:S(2)}) collective-permute-start(bf16[512,3072]{1,0:T(8,128)(2,1)S(1)} %reorder_hidden.1.own_ref), channel_id=1, source_target_pairs={{0,1},{1,0},{2,3},{3,2},{4,5},{5,4},{6,7},{7,6},{8,9},{9,8},{10,11... | collective-permute-start | bytes 9437192 | tf_op jit(solution)/shard_map/ppermute | solution.py:432
  22.1 0.9 reshape.436
  23.4 1.0 broadcast_in_dim.35
  24.3 7.8 %all-to-all-start.1 = ((bf16[16,48,512]{2,1,0:T(8,128)(2,1)}), bf16[16,48,512]{2,1,0:T(8,128)(2,1)}, u32[]{:S(2)}, u32[]{:S(2)}) async-start(bf16[16,48,512]{2,1,0:T(8,128)(2,1)} %broadcast_in_dim.35), calls=%async_computation.1 | async-start | bytes 1572864 | tf_op jit(solution)/shard_map/all_to_all | solution.py:328
  32.2 0.8 copy.20
  33.0 22.5 %all-to-all-done.1 = bf16[16,48,512]{2,1,0:T(8,128)(2,1)} async-done(((bf16[16,48,512]{2,1,0:T(8,128)(2,1)}), bf16[16,48,512]{2,1,0:T(8,128)(2,1)}, u32[]{:S(2)}, u32[]{:S(2)}) %all-to-all-start.1) | async-done | bytes 786464 | tf_op jit(solution)/shard_map/all_to_all | solution.py:328
  55.5 2.0 %halves.1 = (bf16[384,512]{1,0:T(8,128)(2,1)}, bf16[384,512]{1,0:T(8,128)(2,1)}) custom-call(bf16[768,512]{1,0:T(8,128)(2,1)} %bitcast.12.whole_ref), custom_call_target="tpu_custom_call" | custom-call | tf_op jit(solution)/shard_map/halves/pallas_call | solution.py:343
  57.5 3.1 %collective-permute-start.1 = (bf16[384,512]{1,0:T(8,128)(2,1)}, bf16[384,512]{1,0:T(8,128)(2,1)S(1)}, u32[]{:S(2)}, u32[]{:S(2)}) collective-permute-start(bf16[384,512]{1,0:T(8,128)(2,1)} %get-tuple-element.7.rest_0_), channel_id=1, source_target_pairs={{0,8},{8,16},{16,24},{24,0},{1,9},{9,17},{17,25},{25,1},{2,10},{10... | collective-permute-start | bytes 1179656 | tf_op jit(solution)/shard_map/ppermute | solution.py:364
  60.6 3.4 %collective-permute-start.4 = (bf16[384,512]{1,0:T(8,128)(2,1)}, bf16[384,512]{1,0:T(8,128)(2,1)}, u32[]{:S(2)}, u32[]{:S(2)}) collective-permute-start(bf16[384,512]{1,0:T(8,128)(2,1)} %get-tuple-element.8.rest_1_), channel_id=1, source_target_pairs={{0,24},{8,0},{16,8},{24,16},{1,25},{9,1},{17,9},{25,17},{2,26},{10... | collective-permute-start | bytes 1179656 | tf_op jit(solution)/shard_map/ppermute | solution.py:364
  64.2 1.8 %maximum_bitcast_fusion = bf16[8,32,640]{2,1,0:T(8,128)(2,1)} fusion(bf16[32,8,64]{2,0,1:T(8,128)(2,1)S(1)} %broadcast_in_dim.31, bf16[32,8,64]{2,0,1:T(8,128)(2,1)S(1)} %broadcast_in_dim.30, bf16[32,8,512]{2,0,1:T(8,128)(2,1)} %copy.20), kind=kLoop, calls=%fused_computation.4 | loop fusion | flops 983040 | bytes 655360 | tf_op jit(solution)/shard_map/transpose | solution.py:412
  66.0 6.0 %all-to-all-start = ((bf16[8,32,640]{2,1,0:T(8,128)(2,1)}), bf16[8,32,640]{2,1,0:T(8,128)(2,1)}, u32[]{:S(2)}, u32[]{:S(2)}) async-start(bf16[8,32,640]{2,1,0:T(8,128)(2,1)} %maximum_bitcast_fusion), calls=%async_computation | async-start | bytes 655360 | tf_op jit(solution)/shard_map/all_to_all | solution.py:413
  72.1 1.9 %collective-permute-start.2 = (bf16[384,512]{1,0:T(8,128)(2,1)}, bf16[384,512]{1,0:T(8,128)(2,1)S(1)}, u32[]{:S(2)}, u32[]{:S(2)}) collective-permute-start(bf16[384,512]{1,0:T(8,128)(2,1)} %get-tuple-element.8.rest_1_), channel_id=1, source_target_pairs={{0,8},{8,16},{16,24},{24,0},{1,9},{9,17},{17,25},{25,1},{2,10},{10... | collective-permute-start | bytes 1179656 | tf_op jit(solution)/shard_map/ppermute | solution.py:364
  74.0 4.6 %collective-permute-start.3 = (bf16[384,512]{1,0:T(8,128)(2,1)}, bf16[384,512]{1,0:T(8,128)(2,1)S(1)}, u32[]{:S(2)}, u32[]{:S(2)}) collective-permute-start(bf16[384,512]{1,0:T(8,128)(2,1)} %get-tuple-element.7.rest_0_), channel_id=1, source_target_pairs={{0,24},{8,0},{16,8},{24,16},{1,25},{9,1},{17,9},{25,17},{2,26},{10... | collective-permute-start | bytes 1179656 | tf_op jit(solution)/shard_map/ppermute | solution.py:364
  78.6 1.9 %collective-permute-start.5 = (bf16[384,512]{1,0:T(8,128)(2,1)S(1)}, bf16[384,512]{1,0:T(8,128)(2,1)S(1)}, u32[]{:S(2)}, u32[]{:S(2)}) collective-permute-start(bf16[384,512]{1,0:T(8,128)(2,1)S(1)} %collective-permute-done.1.rest_0_), channel_id=1, source_target_pairs={{0,8},{8,16},{16,24},{24,0},{1,9},{9,17},{17,25},{25,1},{2,10},{10... | collective-permute-start | bytes 1179656 | tf_op jit(solution)/shard_map/ppermute | solution.py:364
  80.5 4.6 %collective-permute-start.6 = (bf16[384,512]{1,0:T(8,128)(2,1)}, bf16[384,512]{1,0:T(8,128)(2,1)S(1)}, u32[]{:S(2)}, u32[]{:S(2)}) collective-permute-start(bf16[384,512]{1,0:T(8,128)(2,1)} %collective-permute-done.4.rest_3_), channel_id=1, source_target_pairs={{0,24},{8,0},{16,8},{24,16},{1,25},{9,1},{17,9},{25,17},{2,26},{10... | collective-permute-start | bytes 1179656 | tf_op jit(solution)/shard_map/ppermute | solution.py:364
  85.8 1.9 %fusion = (f32[1024,128]{1,0:T(8,128)S(1)}, f32[1024,128]{1,0:T(8,128)S(1)}) fusion(f32[128]{0:T(128)S(1)} %get-tuple-element.25, f32[128]{0:T(128)S(1)} %get-tuple-element.26, f32[1024]{0:T(1024)S(1)} %fusion.6), kind=kLoop, calls=%fused_computation.3 | loop fusion | flops 262144 | bytes 1053696 | tf_op jit(solution)/shard_map/mul | solution.py:425
  87.7 2.3 %first_product.1.total_ref = f32[1024,512]{1,0:T(8,128)S(1)} custom-call(s32[1]{0:T(128)} %bitcast.5.core_ref, bf16[512,3072]{1,0:T(8,128)(2,1)S(1)} %reorder_hidden.1.own_ref, bf16[512,3072]{1,0:T(8,128)(2,1)} %collective-permute-done.other_ref, bf16[384,512]{1,0:T(8,128)(2,1)} %get-tuple-element.7.rest_0_, bf16[384,512]{1,0:T(8,128)(2,1)} %get-tuple-element.8.rest_1_), custom_call_target="tpu_custom_call" | custom-call | tf_op jit(solution)/shard_map/first_product/pallas_call | solution.py:116
  90.1 3.4 %middle_product.1.total_ref = f32[1024,512]{1,0:T(8,128)S(1)} custom-call(s32[1]{0:T(128)} %bitcast.5.core_ref, bf16[512,3072]{1,0:T(8,128)(2,1)S(1)} %reorder_hidden.1.own_ref, bf16[512,3072]{1,0:T(8,128)(2,1)} %collective-permute-done.other_ref, f32[1024,512]{1,0:T(8,128)S(1)} %first_product.1.total_ref, ...), custom_call_target="tpu_custom_call" | custom-call | tf_op jit(solution)/shard_map/middle_product/pallas_call | solution.py:116
  93.5 1.0 collective-permute-done.5.rest_0_
  94.5 1.0 collective-permute-done.6.rest_1_
  95.5 2.8 %project.1 = bf16[4,1024,128]{2,1,0:T(8,128)(2,1)S(1)} custom-call(s32[1]{0:T(128)} %bitcast.5.core_ref, bf16[512,3072]{1,0:T(8,128)(2,1)S(1)} %reorder_hidden.1.own_ref, bf16[512,3072]{1,0:T(8,128)(2,1)} %collective-permute-done.other_ref, f32[1024,512]{1,0:T(8,128)S(1)} %middle_product.1.total_ref, f32[1024,128]{1,0:T(8,128)S(1)} %get-tuple-element.12.cos_ref, ...), custom_call_target="tpu_custom_call" | custom-call | tf_op jit(solution)/shard_map/project/pallas_call | solution.py:152
  98.3 1.0 copy-done.1
  99.3 4.2 %all-to-all-start.2 = ((bf16[4,1024,128]{2,1,0:T(8,128)(2,1)}), bf16[4,1024,128]{2,1,0:T(8,128)(2,1)S(1)}, u32[]{:S(2)}, u32[]{:S(2)}) async-start(bf16[4,1024,128]{2,1,0:T(8,128)(2,1)} %copy-done.1), calls=%async_computation.2 | async-start | bytes 2097152 | tf_op jit(solution)/shard_map/all_to_all | solution.py:462
  104.6 1.0 slice.28.query_ref
  105.6 1.1 convert_reduce_fusion.1
  108.7 20.1 %all-to-all-done.2 = bf16[4,1024,128]{2,1,0:T(8,128)(2,1)S(1)} async-done(((bf16[4,1024,128]{2,1,0:T(8,128)(2,1)}), bf16[4,1024,128]{2,1,0:T(8,128)(2,1)S(1)}, u32[]{:S(2)}, u32[]{:S(2)}) %all-to-all-start.2) | async-done | bytes 1048608 | tf_op jit(solution)/shard_map/all_to_all | solution.py:462
  128.7 11.5 %attend.1 = bf16[256,512]{1,0:T(8,128)(2,1)S(1)} custom-call(s32[2,8]{1,0:T(2,128)S(1)} %pad_add_fusion.bound_ref, bf16[8,256,128]{2,1,0:T(8,128)(2,1)S(1)} %prepare_queries.1.query_ref, bf16[4096,128]{1,0:T(8,128)(2,1)S(1)} %bitcast.45, s32[8,1,256]{2,1,0:T(1,128)S(1)} %tile.18.last_ref, bf16[256,256]{1,0:T(8,128)(2,1)S(1)} %get-tuple-element.15.unpick_ref), custom_call_target="tpu_custom_call" | custom-call | tf_op jit(solution)/shard_map/attend/pallas_call | solution.py:297
  140.3 12.6 %all_to_all.20 = bf16[8,32,512]{2,1,0:T(8,128)(2,1)S(1)} all-to-all(bf16[8,32,512]{2,1,0:T(8,128)(2,1)S(1)} %bitcast.46), channel_id=1, replica_groups=mesh['yh'=2,'z'=8,'x'=4,'yl'=4,'co'=2] {'yl','co'}, dimensions={0} | all-to-all | bytes 524288 | tf_op jit(solution)/shard_map/all_to_all | solution.py:465
  153.0 0.8 reshape.441
  (56 shorter events, 5.0 us)
Async XLA Ops:
  0.0 0.7 copy-start
  13.1 19.0 %copy-start.2 = (bf16[1,32,4096]{2,1,0:T(8,128)(2,1)S(1)}, bf16[1,32,4096]{2,1,0:T(8,128)(2,1)}, u32[]{:S(2)}) copy-start(bf16[1,32,4096]{2,1,0:T(8,128)(2,1)} %param.10) | copy-start | bytes 786436
  13.1 19.8 %copy-start.5 = (s32[1,32]{1,0:T(1,128)S(1)}, s32[1,32]{1,0:T(1,128)}, u32[]{:S(2)}) copy-start(s32[1,32]{1,0:T(1,128)} %param.12) | copy-start | bytes 388
  13.2 74.5 %collective-permute-start = (bf16[512,3072]{1,0:T(8,128)(2,1)S(1)}, bf16[512,3072]{1,0:T(8,128)(2,1)}, u32[]{:S(2)}, u32[]{:S(2)}) collective-permute-start(bf16[512,3072]{1,0:T(8,128)(2,1)S(1)} %reorder_hidden.1.own_ref), channel_id=1, source_target_pairs={{0,1},{1,0},{2,3},{3,2},{4,5},{5,4},{6,7},{7,6},{8,9},{9,8},{10,11... | collective-permute-start | bytes 9437192 | tf_op jit(solution)/shard_map/ppermute | solution.py:432
  23.3 48.8 %copy-start.3 = (s32[1,512]{1,0:T(1,128)S(1)}, s32[1,512]{1,0:T(1,128)}, u32[]{:S(2)}) copy-start(s32[1,512]{1,0:T(1,128)} %param.11) | copy-start | bytes 6148
  24.3 31.1 %all-to-all-start.1 = ((bf16[16,48,512]{2,1,0:T(8,128)(2,1)}), bf16[16,48,512]{2,1,0:T(8,128)(2,1)}, u32[]{:S(2)}, u32[]{:S(2)}) async-start(bf16[16,48,512]{2,1,0:T(8,128)(2,1)} %broadcast_in_dim.35), calls=%async_computation.1 | async-start | bytes 1572864 | tf_op jit(solution)/shard_map/all_to_all | solution.py:328
  57.5 21.1 %collective-permute-start.1 = (bf16[384,512]{1,0:T(8,128)(2,1)}, bf16[384,512]{1,0:T(8,128)(2,1)S(1)}, u32[]{:S(2)}, u32[]{:S(2)}) collective-permute-start(bf16[384,512]{1,0:T(8,128)(2,1)} %get-tuple-element.7.rest_0_), channel_id=1, source_target_pairs={{0,8},{8,16},{16,24},{24,0},{1,9},{9,17},{17,25},{25,1},{2,10},{10... | collective-permute-start | bytes 1179656 | tf_op jit(solution)/shard_map/ppermute | solution.py:364
  60.6 19.9 %collective-permute-start.4 = (bf16[384,512]{1,0:T(8,128)(2,1)}, bf16[384,512]{1,0:T(8,128)(2,1)}, u32[]{:S(2)}, u32[]{:S(2)}) collective-permute-start(bf16[384,512]{1,0:T(8,128)(2,1)} %get-tuple-element.8.rest_1_), channel_id=1, source_target_pairs={{0,24},{8,0},{16,8},{24,16},{1,25},{9,1},{17,9},{25,17},{2,26},{10... | collective-permute-start | bytes 1179656 | tf_op jit(solution)/shard_map/ppermute | solution.py:364
  66.0 33.3 %all-to-all-start = ((bf16[8,32,640]{2,1,0:T(8,128)(2,1)}), bf16[8,32,640]{2,1,0:T(8,128)(2,1)}, u32[]{:S(2)}, u32[]{:S(2)}) async-start(bf16[8,32,640]{2,1,0:T(8,128)(2,1)} %maximum_bitcast_fusion), calls=%async_computation | async-start | bytes 655360 | tf_op jit(solution)/shard_map/all_to_all | solution.py:413
  72.1 18.0 %collective-permute-start.2 = (bf16[384,512]{1,0:T(8,128)(2,1)}, bf16[384,512]{1,0:T(8,128)(2,1)S(1)}, u32[]{:S(2)}, u32[]{:S(2)}) collective-permute-start(bf16[384,512]{1,0:T(8,128)(2,1)} %get-tuple-element.8.rest_1_), channel_id=1, source_target_pairs={{0,8},{8,16},{16,24},{24,0},{1,9},{9,17},{17,25},{25,1},{2,10},{10... | collective-permute-start | bytes 1179656 | tf_op jit(solution)/shard_map/ppermute | solution.py:364
  74.0 16.1 %collective-permute-start.3 = (bf16[384,512]{1,0:T(8,128)(2,1)}, bf16[384,512]{1,0:T(8,128)(2,1)S(1)}, u32[]{:S(2)}, u32[]{:S(2)}) collective-permute-start(bf16[384,512]{1,0:T(8,128)(2,1)} %get-tuple-element.7.rest_0_), channel_id=1, source_target_pairs={{0,24},{8,0},{16,8},{24,16},{1,25},{9,1},{17,9},{25,17},{2,26},{10... | collective-permute-start | bytes 1179656 | tf_op jit(solution)/shard_map/ppermute | solution.py:364
  78.6 15.9 %collective-permute-start.5 = (bf16[384,512]{1,0:T(8,128)(2,1)S(1)}, bf16[384,512]{1,0:T(8,128)(2,1)S(1)}, u32[]{:S(2)}, u32[]{:S(2)}) collective-permute-start(bf16[384,512]{1,0:T(8,128)(2,1)S(1)} %collective-permute-done.1.rest_0_), channel_id=1, source_target_pairs={{0,8},{8,16},{16,24},{24,0},{1,9},{9,17},{17,25},{25,1},{2,10},{10... | collective-permute-start | bytes 1179656 | tf_op jit(solution)/shard_map/ppermute | solution.py:364
  80.5 15.0 %collective-permute-start.6 = (bf16[384,512]{1,0:T(8,128)(2,1)}, bf16[384,512]{1,0:T(8,128)(2,1)S(1)}, u32[]{:S(2)}, u32[]{:S(2)}) collective-permute-start(bf16[384,512]{1,0:T(8,128)(2,1)} %collective-permute-done.4.rest_3_), channel_id=1, source_target_pairs={{0,24},{8,0},{16,8},{24,16},{1,25},{9,1},{17,9},{25,17},{2,26},{10... | collective-permute-start | bytes 1179656 | tf_op jit(solution)/shard_map/ppermute | solution.py:364
  98.3 1.0 copy-start.1
  99.3 8.0 %copy-start.4 = (f32[128]{0:T(128)S(1)}, f32[128]{0:T(128)}, u32[]{:S(2)}) copy-start(f32[128]{0:T(128)} %constant.108.clone) | copy-start | bytes 1540
  99.3 29.4 %all-to-all-start.2 = ((bf16[4,1024,128]{2,1,0:T(8,128)(2,1)}), bf16[4,1024,128]{2,1,0:T(8,128)(2,1)S(1)}, u32[]{:S(2)}, u32[]{:S(2)}) async-start(bf16[4,1024,128]{2,1,0:T(8,128)(2,1)} %copy-done.1), calls=%async_computation.2 | async-start | bytes 2097152 | tf_op jit(solution)/shard_map/all_to_all | solution.py:462

commit v5 on v4

--- a/solution.py
+++ b/solution.py
@@ -99,31 +99,21 @@
         out_ref[here, :] = product(hidden_ref, pieces)
 
 
-def partial_sum_kernel(core_ref, own_ref, other_ref, total_ref, *rest):
-    pieces, out_ref = rest[:-1], rest[-1]
-    rows = own_ref.shape[0]
-    core = core_ref[0]
-    for hidden_ref, place in ((own_ref, core), (other_ref, 1 - core)):
-        here = pl.ds(pl.multiple_of(place * rows, rows), rows)
-        out_ref[here, :] = total_ref[here, :] + product(hidden_ref, pieces)
-
-
-def partial_product(core, own, other, pieces, *total):
+def partial_product(core, own, other, pieces):
     vmem = pl.BlockSpec(memory_space=pltpu.VMEM)
     rows = own.shape[0]
-    column = 0 if total else 2
-    part = pl.BlockSpec((rows, sum(p.shape[0] for p in pieces)), lambda i: (0, column))
-    return pl.pallas_call(
-        partial_sum_kernel if total else partial_kernel,
+    part = pl.BlockSpec((rows, sum(p.shape[0] for p in pieces)), lambda i: (0, 0))
+    return pl.pallas_call(
+        partial_kernel,
         grid=(1,),
         in_specs=[pl.BlockSpec(memory_space=pltpu.SMEM)]
         + [part, part]
-        + [vmem] * (len(pieces) + len(total)),
+        + [vmem] * len(pieces),
         out_specs=vmem,
         out_shape=jax.ShapeDtypeStruct((2 * rows, pieces[0].shape[1]), jnp.float32),
-        name="middle_product" if total else "first_product",
+        name="partial_product",
         compiler_params=pltpu.CompilerParams(vmem_limit_bytes=18 << 20),
-    )(core, own, other, *total, *pieces)
+    )(core, own, other, *pieces)
 
 
 def project_kernel(core_ref, own_ref, other_ref, total_ref, cos_ref, sin_ref, *rest):
@@ -322,19 +312,26 @@
     ]
 
 
-def spread(x):
-    groups = mirrored_groups()
-    copies = jnp.broadcast_to(x[None], (len(groups[0]),) + x.shape)
+def spread(copies):
     whole = lax.all_to_all(
-        copies, ("yh", "z", "yl"), 0, 0, axis_index_groups=groups, tiled=True
-    )
-    return whole.reshape((-1,) + x.shape[1:])
-
-
-def halves_kernel(whole_ref, low_ref, high_ref):
+        copies,
+        ("yh", "z", "yl"),
+        0,
+        0,
+        axis_index_groups=mirrored_groups(),
+        tiled=True,
+    )
+    return whole.reshape(-1, copies.shape[2])
+
+
+def halves_kernel(whole_ref, low_ref, high_ref, low_sem, high_sem):
     half = low_ref.shape[0]
-    low_ref[...] = whole_ref[:half]
-    high_ref[...] = whole_ref[half:]
+    low = pltpu.make_async_copy(whole_ref.at[pl.ds(0, half)], low_ref, low_sem)
+    high = pltpu.make_async_copy(whole_ref.at[pl.ds(half, half)], high_ref, high_sem)
+    low.start()
+    high.start()
+    low.wait()
+    high.wait()
 
 
 def halves(whole):
@@ -342,21 +339,45 @@
     shape = jax.ShapeDtypeStruct((whole.shape[0] // 2, whole.shape[1]), whole.dtype)
     return pl.pallas_call(
         halves_kernel,
-        in_specs=[vmem],
+        in_specs=[pl.BlockSpec(memory_space=pl.ANY)],
         out_specs=[vmem, vmem],
         out_shape=[shape, shape],
+        scratch_shapes=[pltpu.SemaphoreType.DMA, pltpu.SemaphoreType.DMA],
         name="halves",
+        compiler_params=pltpu.CompilerParams(vmem_limit_bytes=4 << 20),
+    )(whole)
+
+
+def copies_kernel(core_ref, blocks_ref, out_ref, mine_ref):
+    block_rows = blocks_ref.shape[0]
+    mine_ref[...] = jnp.zeros_like(mine_ref)
+    for head in range(KV_HEADS // 2):
+        column = pl.multiple_of((2 * head + core_ref[0]) * LANES, LANES)
+        mine_ref[:block_rows, head * LANES : (head + 1) * LANES] = blocks_ref[
+            :, pl.ds(column, LANES)
+        ]
+    for place in range(out_ref.shape[0]):
+        out_ref[place] = mine_ref[...]
+
+
+def weight_copies(blocks, core, count):
+    vmem = pl.BlockSpec(memory_space=pltpu.VMEM)
+    width = blocks.shape[1] // 2
+    return pl.pallas_call(
+        copies_kernel,
+        in_specs=[pl.BlockSpec(memory_space=pltpu.SMEM), vmem],
+        out_specs=vmem,
+        out_shape=jax.ShapeDtypeStruct((count, PAD_ROWS, width), blocks.dtype),
+        scratch_shapes=[pltpu.VMEM((PAD_ROWS, width), blocks.dtype)],
+        name="weight_copies",
         compiler_params=pltpu.CompilerParams(vmem_limit_bytes=6 << 20),
-    )(whole)
+    )(core.reshape(1), blocks)
 
 
 def gather_weight(blocks):
-    block_rows = blocks.shape[0]
-    core = lax.axis_index("co")
-    split = blocks.reshape(block_rows, KV_HEADS // 2, 2, LANES)
-    mine = lax.dynamic_index_in_dim(split, core, 2, False).reshape(block_rows, -1)
-    mine = jnp.pad(mine, ((0, PAD_ROWS - block_rows), (0, 0)))
-    plane = spread(mine)
+    count = lax.axis_size("yh") * lax.axis_size("z")
+    copies = weight_copies(blocks, lax.axis_index("co"), count)
+    plane = spread(copies)
     up, down = ring(4, 1), ring(4, -1)
     low, high = halves(plane)
 
@@ -456,8 +477,7 @@
     prepared = prepare(query, pick, jnp.cos(query_angle), jnp.sin(query_angle) * sign)
 
     place = core.reshape(1)
-    total = partial_product(place, own, other, plane)
-    total = partial_product(place, own, other, middle, total)
+    total = partial_product(place, own, other, middle + plane)
     kv = project(place, own, other, far, total, key_cosine, key_sine)
     kv = lax.all_to_all(kv, "yl", 0, 0, tiled=True).reshape(keys, LANES)
     context = attend(bounds, prepared, kv, last_rows, unpick)

time: 156 us -> 154 us (0.987)
    unnamed x16 -> x18, local copies, waits for them, and re-layouts: 4.82 us -> 5.68 us
  transfers between devices with their start and end apart: 10 -> 10, of which waited for: 4 -> 4; matrix products, arithmetic and copies ran while one was open for 8% -> 6% of each run, Pallas kernels for 7% -> 7%
where the time goes in v5:
time: 154 us; the launch traced here: 152 us
  starting transfers between devices  46.2 us (30%)
  waiting for transfers between devices  45.5 us (30%)
  Pallas kernels  29.4 us (19%)
  blocking collectives  12.6 us (8%)
  local copies, waits for them, and re-layouts  10.5 us (7%)
  other arithmetic  6.89 us (4%)
    all_to_all x1, waiting for transfers between devices, spread(): lax.all_to_all(copies, ('yh', 'z', 'yl'), 0, 0, axis_index_groups=mirrore...  22.5 us
    all_to_all x1, waiting for transfers between devices, attention(): kv = lax.all_to_all(kv, 'yl', 0, 0, tiled=True).reshape(keys, LANES)  20.1 us
    ppermute x6, starting transfers between devices, send(): return lax.ppermute(piece, 'x', pairs)  19.5 us
    all_to_all x1, blocking collectives, attention(): context = lax.all_to_all(context, SEQ, 0, 0, tiled=True)  12.6 us
    pallas_call x1, Pallas kernels, attend(): pl.pallas_call(attend_kernel, in_specs=[pl.BlockSpec(memory_space=pltpu.S...  11.5 us
    ppermute x1, starting transfers between devices, attention(): other = lax.ppermute(own, 'co', ring(2, 1))  8.76 us
    pallas_call x1, Pallas kernels, reorder(): pl.pallas_call(reorder_kernel, grid=(columns // tile,), in_specs=[pl.Bloc...  7.93 us
    all_to_all x1, starting transfers between devices, spread(): lax.all_to_all(copies, ('yh', 'z', 'yl'), 0, 0, axis_index_groups=mirrore...  7.75 us
  transfers between devices with their start and end apart: 10, of which 4 were waited for; matrix products, arithmetic and copies ran while one was open for 6% of the time, Pallas kernels for 7%

profile of v5, /device:TPU:1, one launch (start us, length us, event | category | flops | bytes accessed | tf_op | source)
XLA Modules:
  0.0 152.1 jit_solution(13831861476940173836)
XLA Ops:
  0.7 0.8 gather_fusion
  1.6 3.3 %copy.19 = bf16[1,512,2880]{2,1,0:T(8,128)(2,1)S(1)} copy(bf16[1,512,2880]{1,2,0:T(8,128)(2,1)} %param.7) | data formatting | bytes 5898240 | tf_op args[0]
  5.2 7.9 %reorder_hidden.1.own_ref = bf16[512,3072]{1,0:T(8,128)(2,1)S(1)} custom-call(s32[64]{0:T(128)S(1)} %get-tuple-element.20.window_ref, s32[1,3072]{1,0:T(1,128)S(1)} %select_n.101.source_ref, bf16[512,2944]{1,0:T(8,128)(2,1)S(1)} %pad.4.hidden_ref), custom_call_target="tpu_custom_call" | custom-call | tf_op jit(solution)/shard_map/reorder_hidden/pallas_call | solution.py:64
  13.2 8.8 %collective-permute-start = (bf16[512,3072]{1,0:T(8,128)(2,1)S(1)}, bf16[512,3072]{1,0:T(8,128)(2,1)}, u32[]{:S(2)}, u32[]{:S(2)}) collective-permute-start(bf16[512,3072]{1,0:T(8,128)(2,1)S(1)} %reorder_hidden.1.own_ref), channel_id=1, source_target_pairs={{0,1},{1,0},{2,3},{3,2},{4,5},{5,4},{6,7},{7,6},{8,9},{9,8},{10,11... | collective-permute-start | bytes 9437192 | tf_op jit(solution)/shard_map/ppermute | solution.py:453
  22.1 0.9 copy-done.2
  22.9 7.8 %all-to-all-start.1 = ((bf16[16,48,512]{2,1,0:T(8,128)(2,1)}), bf16[16,48,512]{2,1,0:T(8,128)(2,1)}, u32[]{:S(2)}, u32[]{:S(2)}) async-start(bf16[16,48,512]{2,1,0:T(8,128)(2,1)} %copy-done.2), calls=%async_computation.1 | async-start | bytes 1572864 | tf_op jit(solution)/shard_map/all_to_all | solution.py:316
  30.8 0.8 copy.18
  31.6 22.5 %all-to-all-done.1 = bf16[16,48,512]{2,1,0:T(8,128)(2,1)} async-done(((bf16[16,48,512]{2,1,0:T(8,128)(2,1)}), bf16[16,48,512]{2,1,0:T(8,128)(2,1)}, u32[]{:S(2)}, u32[]{:S(2)}) %all-to-all-start.1) | async-done | bytes 786464 | tf_op jit(solution)/shard_map/all_to_all | solution.py:316
  54.1 1.9 %halves.1 = (bf16[384,512]{1,0:T(8,128)(2,1)S(1)}, bf16[384,512]{1,0:T(8,128)(2,1)}) custom-call(bf16[768,512]{1,0:T(8,128)(2,1)} %bitcast.12.whole_ref), custom_call_target="tpu_custom_call" | custom-call | tf_op jit(solution)/shard_map/halves/pallas_call | solution.py:340
  56.0 3.1 %collective-permute-start.1 = (bf16[384,512]{1,0:T(8,128)(2,1)S(1)}, bf16[384,512]{1,0:T(8,128)(2,1)}, u32[]{:S(2)}, u32[]{:S(2)}) collective-permute-start(bf16[384,512]{1,0:T(8,128)(2,1)S(1)} %get-tuple-element.7.rest_4_), channel_id=1, source_target_pairs={{0,8},{8,16},{16,24},{24,0},{1,9},{9,17},{17,25},{25,1},{2,10},{10... | collective-permute-start | bytes 1179656 | tf_op jit(solution)/shard_map/ppermute | solution.py:385
  59.1 3.4 %collective-permute-start.4 = (bf16[384,512]{1,0:T(8,128)(2,1)}, bf16[384,512]{1,0:T(8,128)(2,1)}, u32[]{:S(2)}, u32[]{:S(2)}) collective-permute-start(bf16[384,512]{1,0:T(8,128)(2,1)} %get-tuple-element.8.rest_5_), channel_id=1, source_target_pairs={{0,24},{8,0},{16,8},{24,16},{1,25},{9,1},{17,9},{25,17},{2,26},{10... | collective-permute-start | bytes 1179656 | tf_op jit(solution)/shard_map/ppermute | solution.py:385
  62.6 1.8 %maximum_bitcast_fusion = bf16[8,32,640]{2,1,0:T(8,128)(2,1)} fusion(bf16[32,8,64]{2,0,1:T(8,128)(2,1)S(1)} %broadcast_in_dim.29, bf16[32,8,64]{2,0,1:T(8,128)(2,1)S(1)} %broadcast_in_dim.28, bf16[32,8,512]{2,0,1:T(8,128)(2,1)} %copy.18), kind=kLoop, calls=%fused_computation.4 | loop fusion | flops 983040 | bytes 655360 | tf_op jit(solution)/shard_map/transpose | solution.py:433
  64.4 6.0 %all-to-all-start = ((bf16[8,32,640]{2,1,0:T(8,128)(2,1)}), bf16[8,32,640]{2,1,0:T(8,128)(2,1)}, u32[]{:S(2)}, u32[]{:S(2)}) async-start(bf16[8,32,640]{2,1,0:T(8,128)(2,1)} %maximum_bitcast_fusion), calls=%async_computation | async-start | bytes 655360 | tf_op jit(solution)/shard_map/all_to_all | solution.py:434
  70.6 1.9 %collective-permute-start.2 = (bf16[384,512]{1,0:T(8,128)(2,1)}, bf16[384,512]{1,0:T(8,128)(2,1)S(1)}, u32[]{:S(2)}, u32[]{:S(2)}) collective-permute-start(bf16[384,512]{1,0:T(8,128)(2,1)} %get-tuple-element.8.rest_5_), channel_id=1, source_target_pairs={{0,8},{8,16},{16,24},{24,0},{1,9},{9,17},{17,25},{25,1},{2,10},{10... | collective-permute-start | bytes 1179656 | tf_op jit(solution)/shard_map/ppermute | solution.py:385
  72.5 4.6 %collective-permute-start.3 = (bf16[384,512]{1,0:T(8,128)(2,1)S(1)}, bf16[384,512]{1,0:T(8,128)(2,1)S(1)}, u32[]{:S(2)}, u32[]{:S(2)}) collective-permute-start(bf16[384,512]{1,0:T(8,128)(2,1)S(1)} %get-tuple-element.7.rest_4_), channel_id=1, source_target_pairs={{0,24},{8,0},{16,8},{24,16},{1,25},{9,1},{17,9},{25,17},{2,26},{10... | collective-permute-start | bytes 1179656 | tf_op jit(solution)/shard_map/ppermute | solution.py:385
  77.1 1.9 %collective-permute-start.5 = (bf16[384,512]{1,0:T(8,128)(2,1)}, bf16[384,512]{1,0:T(8,128)(2,1)S(1)}, u32[]{:S(2)}, u32[]{:S(2)}) collective-permute-start(bf16[384,512]{1,0:T(8,128)(2,1)} %collective-permute-done.1.rest_0_), channel_id=1, source_target_pairs={{0,8},{8,16},{16,24},{24,0},{1,9},{9,17},{17,25},{25,1},{2,10},{10... | collective-permute-start | bytes 1179656 | tf_op jit(solution)/shard_map/ppermute | solution.py:385
  79.0 4.6 %collective-permute-start.6 = (bf16[384,512]{1,0:T(8,128)(2,1)}, bf16[384,512]{1,0:T(8,128)(2,1)S(1)}, u32[]{:S(2)}, u32[]{:S(2)}) collective-permute-start(bf16[384,512]{1,0:T(8,128)(2,1)} %collective-permute-done.4.rest_3_), channel_id=1, source_target_pairs={{0,24},{8,0},{16,8},{24,16},{1,25},{9,1},{17,9},{25,17},{2,26},{10... | collective-permute-start | bytes 1179656 | tf_op jit(solution)/shard_map/ppermute | solution.py:385
  83.6 0.7 compare_select_fusion.12
  84.3 1.9 %fusion = (f32[1024,128]{1,0:T(8,128)S(1)}, f32[1024,128]{1,0:T(8,128)S(1)}) fusion(f32[128]{0:T(128)S(1)} %get-tuple-element.25, f32[128]{0:T(128)S(1)} %get-tuple-element.26, f32[1024]{0:T(1024)S(1)} %fusion.6), kind=kLoop, calls=%fused_computation.3 | loop fusion | flops 262144 | bytes 1053696 | tf_op jit(solution)/shard_map/mul | solution.py:446
  86.2 4.6 %partial_product.1.total_ref = f32[1024,512]{1,0:T(8,128)S(1)} custom-call(s32[1]{0:T(128)} %bitcast.5.core_ref, bf16[512,3072]{1,0:T(8,128)(2,1)S(1)} %reorder_hidden.1.own_ref, bf16[512,3072]{1,0:T(8,128)(2,1)} %collective-permute-done.other_ref, bf16[384,512]{1,0:T(8,128)(2,1)} %collective-permute-done.1.rest_0_, ...), custom_call_target="tpu_custom_call" | custom-call | tf_op jit(solution)/shard_map/partial_product/pallas_call | solution.py:106
  90.8 2.2 %collective-permute-done.5.rest_0_ = bf16[384,512]{1,0:T(8,128)(2,1)S(1)} collective-permute-done((bf16[384,512]{1,0:T(8,128)(2,1)}, bf16[384,512]{1,0:T(8,128)(2,1)S(1)}, u32[]{:S(2)}, u32[]{:S(2)}) %collective-permute-start.5) | collective-permute-done | bytes 393248 | tf_op jit(solution)/shard_map/ppermute | solution.py:385
  93.0 0.8 collective-permute-done.6.rest_1_
  93.8 2.8 %project.1 = bf16[4,1024,128]{2,1,0:T(8,128)(2,1)S(1)} custom-call(s32[1]{0:T(128)} %bitcast.5.core_ref, bf16[512,3072]{1,0:T(8,128)(2,1)S(1)} %reorder_hidden.1.own_ref, bf16[512,3072]{1,0:T(8,128)(2,1)} %collective-permute-done.other_ref, f32[1024,512]{1,0:T(8,128)S(1)} %partial_product.1.total_ref, f32[1024,128]{1,0:T(8,128)S(1)} %get-tuple-element.12.cos_ref, ...), custom_call_target="tpu_custom_call" | custom-call | tf_op jit(solution)/shard_map/project/pallas_call | solution.py:142
  96.6 1.0 copy-done.1
  97.5 4.2 %all-to-all-start.2 = ((bf16[4,1024,128]{2,1,0:T(8,128)(2,1)}), bf16[4,1024,128]{2,1,0:T(8,128)(2,1)S(1)}, u32[]{:S(2)}, u32[]{:S(2)}) async-start(bf16[4,1024,128]{2,1,0:T(8,128)(2,1)} %copy-done.1), calls=%async_computation.2 | async-start | bytes 2097152 | tf_op jit(solution)/shard_map/all_to_all | solution.py:482
  102.9 1.0 slice.28.query_ref
  103.8 1.1 convert_reduce_fusion.1
  106.1 0.6 prepare_queries.1.query_ref
  106.9 20.1 %all-to-all-done.2 = bf16[4,1024,128]{2,1,0:T(8,128)(2,1)S(1)} async-done(((bf16[4,1024,128]{2,1,0:T(8,128)(2,1)}), bf16[4,1024,128]{2,1,0:T(8,128)(2,1)S(1)}, u32[]{:S(2)}, u32[]{:S(2)}) %all-to-all-start.2) | async-done | bytes 1048608 | tf_op jit(solution)/shard_map/all_to_all | solution.py:482
  127.0 11.5 %attend.1 = bf16[256,512]{1,0:T(8,128)(2,1)S(1)} custom-call(s32[2,8]{1,0:T(2,128)S(1)} %pad_add_fusion.bound_ref, bf16[8,256,128]{2,1,0:T(8,128)(2,1)S(1)} %prepare_queries.1.query_ref, bf16[4096,128]{1,0:T(8,128)(2,1)S(1)} %bitcast.42, s32[8,1,256]{2,1,0:T(1,128)S(1)} %tile.18.last_ref, bf16[256,256]{1,0:T(8,128)(2,1)S(1)} %get-tuple-element.15.unpick_ref), custom_call_target="tpu_custom_call" | custom-call | tf_op jit(solution)/shard_map/attend/pallas_call | solution.py:287
  138.5 12.6 %all_to_all.20 = bf16[8,32,512]{2,1,0:T(8,128)(2,1)S(1)} all-to-all(bf16[8,32,512]{2,1,0:T(8,128)(2,1)S(1)} %bitcast.43), channel_id=1, replica_groups=mesh['yh'=2,'z'=8,'x'=4,'yl'=4,'co'=2] {'yl','co'}, dimensions={0} | all-to-all | bytes 524288 | tf_op jit(solution)/shard_map/all_to_all | solution.py:485
  151.3 0.8 reshape.432
  (54 shorter events, 3.5 us)
Async XLA Ops:
  0.0 0.7 copy-start
  5.2 16.8 %copy-start.3 = (bf16[45,1024]{1,0:T(8,128)(2,1)S(1)}, bf16[45,1024]{1,0:T(8,128)(2,1)}, u32[]{:S(2)}) copy-start(bf16[45,1024]{1,0:T(8,128)(2,1)} %blocks_ref.1) | copy-start | bytes 276484
  5.2 25.5 %copy-start.4 = (bf16[1,32,4096]{2,1,0:T(8,128)(2,1)S(1)}, bf16[1,32,4096]{2,1,0:T(8,128)(2,1)}, u32[]{:S(2)}) copy-start(bf16[1,32,4096]{2,1,0:T(8,128)(2,1)} %param.10) | copy-start | bytes 786436
  13.2 18.4 %copy-start.7 = (s32[1,32]{1,0:T(1,128)S(1)}, s32[1,32]{1,0:T(1,128)}, u32[]{:S(2)}) copy-start(s32[1,32]{1,0:T(1,128)} %param.12) | copy-start | bytes 388
  13.2 57.4 %copy-start.5 = (s32[1,512]{1,0:T(1,128)S(1)}, s32[1,512]{1,0:T(1,128)}, u32[]{:S(2)}) copy-start(s32[1,512]{1,0:T(1,128)} %param.11) | copy-start | bytes 6148
  13.2 73.0 %collective-permute-start = (bf16[512,3072]{1,0:T(8,128)(2,1)S(1)}, bf16[512,3072]{1,0:T(8,128)(2,1)}, u32[]{:S(2)}, u32[]{:S(2)}) collective-permute-start(bf16[512,3072]{1,0:T(8,128)(2,1)S(1)} %reorder_hidden.1.own_ref), channel_id=1, source_target_pairs={{0,1},{1,0},{2,3},{3,2},{4,5},{5,4},{6,7},{7,6},{8,9},{9,8},{10,11... | collective-permute-start | bytes 9437192 | tf_op jit(solution)/shard_map/ppermute | solution.py:453
  22.0 0.9 copy-start.2
  22.9 31.1 %all-to-all-start.1 = ((bf16[16,48,512]{2,1,0:T(8,128)(2,1)}), bf16[16,48,512]{2,1,0:T(8,128)(2,1)}, u32[]{:S(2)}, u32[]{:S(2)}) async-start(bf16[16,48,512]{2,1,0:T(8,128)(2,1)} %copy-done.2), calls=%async_computation.1 | async-start | bytes 1572864 | tf_op jit(solution)/shard_map/all_to_all | solution.py:316
  56.0 21.1 %collective-permute-start.1 = (bf16[384,512]{1,0:T(8,128)(2,1)S(1)}, bf16[384,512]{1,0:T(8,128)(2,1)}, u32[]{:S(2)}, u32[]{:S(2)}) collective-permute-start(bf16[384,512]{1,0:T(8,128)(2,1)S(1)} %get-tuple-element.7.rest_4_), channel_id=1, source_target_pairs={{0,8},{8,16},{16,24},{24,0},{1,9},{9,17},{17,25},{25,1},{2,10},{10... | collective-permute-start | bytes 1179656 | tf_op jit(solution)/shard_map/ppermute | solution.py:385
  59.1 19.9 %collective-permute-start.4 = (bf16[384,512]{1,0:T(8,128)(2,1)}, bf16[384,512]{1,0:T(8,128)(2,1)}, u32[]{:S(2)}, u32[]{:S(2)}) collective-permute-start(bf16[384,512]{1,0:T(8,128)(2,1)} %get-tuple-element.8.rest_5_), channel_id=1, source_target_pairs={{0,24},{8,0},{16,8},{24,16},{1,25},{9,1},{17,9},{25,17},{2,26},{10... | collective-permute-start | bytes 1179656 | tf_op jit(solution)/shard_map/ppermute | solution.py:385
  64.4 33.1 %all-to-all-start = ((bf16[8,32,640]{2,1,0:T(8,128)(2,1)}), bf16[8,32,640]{2,1,0:T(8,128)(2,1)}, u32[]{:S(2)}, u32[]{:S(2)}) async-start(bf16[8,32,640]{2,1,0:T(8,128)(2,1)} %maximum_bitcast_fusion), calls=%async_computation | async-start | bytes 655360 | tf_op jit(solution)/shard_map/all_to_all | solution.py:434
  70.6 15.6 %collective-permute-start.2 = (bf16[384,512]{1,0:T(8,128)(2,1)}, bf16[384,512]{1,0:T(8,128)(2,1)S(1)}, u32[]{:S(2)}, u32[]{:S(2)}) collective-permute-start(bf16[384,512]{1,0:T(8,128)(2,1)} %get-tuple-element.8.rest_5_), channel_id=1, source_target_pairs={{0,8},{8,16},{16,24},{24,0},{1,9},{9,17},{17,25},{25,1},{2,10},{10... | collective-permute-start | bytes 1179656 | tf_op jit(solution)/shard_map/ppermute | solution.py:385
  72.5 13.7 %collective-permute-start.3 = (bf16[384,512]{1,0:T(8,128)(2,1)S(1)}, bf16[384,512]{1,0:T(8,128)(2,1)S(1)}, u32[]{:S(2)}, u32[]{:S(2)}) collective-permute-start(bf16[384,512]{1,0:T(8,128)(2,1)S(1)} %get-tuple-element.7.rest_4_), channel_id=1, source_target_pairs={{0,24},{8,0},{16,8},{24,16},{1,25},{9,1},{17,9},{25,17},{2,26},{10... | collective-permute-start | bytes 1179656 | tf_op jit(solution)/shard_map/ppermute | solution.py:385
  77.1 15.9 %collective-permute-start.5 = (bf16[384,512]{1,0:T(8,128)(2,1)}, bf16[384,512]{1,0:T(8,128)(2,1)S(1)}, u32[]{:S(2)}, u32[]{:S(2)}) collective-permute-start(bf16[384,512]{1,0:T(8,128)(2,1)} %collective-permute-done.1.rest_0_), channel_id=1, source_target_pairs={{0,8},{8,16},{16,24},{24,0},{1,9},{9,17},{17,25},{25,1},{2,10},{10... | collective-permute-start | bytes 1179656 | tf_op jit(solution)/shard_map/ppermute | solution.py:385
  79.0 14.7 %collective-permute-start.6 = (bf16[384,512]{1,0:T(8,128)(2,1)}, bf16[384,512]{1,0:T(8,128)(2,1)S(1)}, u32[]{:S(2)}, u32[]{:S(2)}) collective-permute-start(bf16[384,512]{1,0:T(8,128)(2,1)} %collective-permute-done.4.rest_3_), channel_id=1, source_target_pairs={{0,24},{8,0},{16,8},{24,16},{1,25},{9,1},{17,9},{25,17},{2,26},{10... | collective-permute-start | bytes 1179656 | tf_op jit(solution)/shard_map/ppermute | solution.py:385
  96.6 1.0 copy-start.1
  97.5 8.0 %copy-start.6 = (f32[128]{0:T(128)S(1)}, f32[128]{0:T(128)}, u32[]{:S(2)}) copy-start(f32[128]{0:T(128)} %constant.104.clone) | copy-start | bytes 1540
  97.5 29.5 %all-to-all-start.2 = ((bf16[4,1024,128]{2,1,0:T(8,128)(2,1)}), bf16[4,1024,128]{2,1,0:T(8,128)(2,1)S(1)}, u32[]{:S(2)}, u32[]{:S(2)}) async-start(bf16[4,1024,128]{2,1,0:T(8,128)(2,1)} %copy-done.1), calls=%async_computation.2 | async-start | bytes 2097152 | tf_op jit(solution)/shard_map/all_to_all | solution.py:482
